TPU v7x, 512 devices: a whole 4x4x16 slice. The times are simulated.
512 devices in a mesh: dp: 128 (over z, x, core), mp: 4 (over y).
Axes of the slice: x: 4, y: 4, z: 16, core: 2. Of those that a mesh axis runs over, the one named last changes fastest.
Arguments:
- patches: bfloat16 [131072, 1408], P('dp', 'mp'), may hold values from -6 to 6
- counts: int32 [128, 4, 4], P('dp'), may hold values from 32 to 64, as said below
- qkv_weight: bfloat16 [1408, 2112], P(None, 'mp')
- grad_context: bfloat16 [131072, 704], P('dp', 'mp'), may hold values from -6 to 6
Outputs:
- grad_patches: bfloat16 [131072, 1408], P('dp', 'mp')
- grad_weight: bfloat16 [1408, 2112], P(None, 'mp')
Inputs may be any that keep to these rules, and one draw needn't show every extreme that they name: `counts`: in every draw one bundle holds 4 images of 64 patches, so a bundle's images fill at most 256 slots.
All inputs are finite; a program needn't handle non-finite values.
Results may differ from a plain program's by a relative error of at most 0.0065.
The roundings to bfloat16 on the way count: a program that leaves them out, or rounds other values in their place, can miss the bound.
Values may be sent and summed in bfloat16 or wider, within the bound.
A program may use at most 64 MiB of HBM per device.

v0:
```python
import math

import jax
import jax.numpy as jnp
from jax import lax
from jax.sharding import PartitionSpec as P

HD = 88
IMGS = 4
BUNDLES = 4
CAP = 256
SEQ = 1024


def from_behind(block, axis, distance):
    devices = range(lax.axis_size(axis))
    route = [((i - distance) % len(devices), i) for i in devices]
    return lax.ppermute(block, axis, route)


def shift_list(n_dp):
    stride = n_dp // BUNDLES
    return [stride // 2 + bundle * stride for bundle in range(BUNDLES)]


def layout(counts_here):
    image_ends = jnp.cumsum(counts_here, axis=1)
    position = jnp.arange(CAP, dtype=jnp.int32)
    segment = jnp.sum((position[None, :, None] >= image_ends[:, None, :]).astype(jnp.int32), axis=2)
    is_valid = segment < IMGS
    same_image = segment[:, :, None] == segment[:, None, :]
    diagonal = position[:, None] == position[None, :]
    allowed = jnp.where(is_valid[:, :, None], same_image, diagonal[None])
    return (is_valid, allowed)


def bring(blocks, n_dp):
    shifts = shift_list(n_dp)
    placed = []
    for bundle in range(BUNDLES):
        placed.append(from_behind(blocks[bundle], "dp", n_dp - shifts[bundle]))
    return jnp.stack(placed)


def send_back(blocks, n_dp):
    shifts = shift_list(n_dp)
    placed = []
    for bundle in range(BUNDLES):
        placed.append(from_behind(blocks[bundle], "dp", shifts[bundle]))
    return jnp.stack(placed)


def shards(patches, counts, qkv_weight, grad_context):
    n_dp = lax.axis_size("dp")
    norm_factor = 1.0 / math.sqrt(n_dp)
    feat = patches.shape[1]
    width = qkv_weight.shape[1]
    heads_here = width // (3 * HD)
    blocks = patches.reshape(BUNDLES, CAP, feat)
    local_rows = bring(blocks, n_dp).reshape(SEQ, feat)
    seq_rows = lax.all_gather(local_rows, "mp", axis=1, tiled=True)
    full_weight = lax.all_gather(qkv_weight, "mp", axis=1, tiled=True)
    packed = jnp.dot(seq_rows, qkv_weight, preferred_element_type=jnp.float32).astype(jnp.bfloat16)
    packed = packed.reshape(BUNDLES, CAP, heads_here, 3, HD)
    queries = packed[:, :, :, 0]
    key_rows = packed[:, :, :, 1]
    value_rows = packed[:, :, :, 2]
    is_valid, allowed = layout(counts[0])
    scale = 1.0 / math.sqrt(HD)
    scores = (
        jnp.einsum("bqhd,bkhd->bhqk", queries, key_rows, preferred_element_type=jnp.float32) * scale
    )
    masked = jnp.where(allowed[:, None], scores, -1e30)
    top = jnp.max(masked, axis=-1, keepdims=True)
    exponent = jnp.where(allowed[:, None], jnp.exp(masked - top), 0.0)
    attn_probs = exponent / jnp.sum(exponent, axis=-1, keepdims=True)
    probs_low = attn_probs.astype(jnp.bfloat16)
    upstream = grad_context.reshape(BUNDLES, CAP, heads_here, HD) * is_valid[
        :, :, None, None
    ].astype(jnp.bfloat16)
    grad_probs = jnp.einsum(
        "bqhd,bkhd->bhqk", upstream, value_rows, preferred_element_type=jnp.float32
    )
    grad_values = jnp.einsum(
        "bhqk,bqhd->bkhd", probs_low, upstream, preferred_element_type=jnp.float32
    ).astype(jnp.bfloat16)
    row_dot = jnp.sum(attn_probs * grad_probs, axis=-1, keepdims=True)
    grad_logits = (attn_probs * (grad_probs - row_dot) * scale).astype(jnp.bfloat16)
    grad_queries = jnp.einsum(
        "bhqk,bkhd->bqhd", grad_logits, key_rows, preferred_element_type=jnp.float32
    ).astype(jnp.bfloat16)
    grad_keys = jnp.einsum(
        "bhqk,bqhd->bkhd", grad_logits, queries, preferred_element_type=jnp.float32
    ).astype(jnp.bfloat16)
    grad_packed = jnp.stack([grad_queries, grad_keys, grad_values], axis=3).reshape(SEQ, width)
    weight_term = lax.dot_general(
        seq_rows, grad_packed, (((0,), (0,)), ((), ())), preferred_element_type=jnp.float32
    )
    grad_weight = (lax.psum(weight_term, "dp") * norm_factor).astype(jnp.bfloat16)
    grad_all = lax.all_gather(grad_packed, "mp", axis=1, tiled=True)
    weight_here = lax.dynamic_slice_in_dim(full_weight, lax.axis_index("mp") * feat, feat, 0)
    grad_local = lax.dot_general(
        grad_all, weight_here, (((1,), (1,)), ((), ())), preferred_element_type=jnp.float32
    ).astype(jnp.bfloat16)
    grad_patches = send_back(grad_local.reshape(BUNDLES, CAP, feat), n_dp).reshape(SEQ, feat)
    return (grad_patches, grad_weight)


def solution(mesh):
    in_specs = (P("dp", "mp"), P("dp", None, None), P(None, "mp"), P("dp", "mp"))
    out_specs = (P("dp", "mp"), P(None, "mp"))
    return jax.shard_map(shards, mesh=mesh, in_specs=in_specs, out_specs=out_specs, check_vma=False)
```

profile of v0, /device:TPU:1, one launch (start us, length us, event | category | flops | bytes accessed | tf_op | source)
XLA Modules:
  0.0 622.8 jit_solution(12078864836297339776)
XLA Ops:
  7.2 0.0 all-gather.4.cloned.1.call-start
  7.2 1.2 fusion.50
  8.5 12.4 %collective-permute-start = (bf16[256,352]{0,1:T(8,128)(2,1)S(1)}, bf16[256,352]{0,1:T(8,128)(2,1)S(1)}, u32[]{:S(2)}, u32[]{:S(2)}) collective-permute-start(bf16[256,352]{0,1:T(8,128)(2,1)S(1)} %get-tuple-element.11), channel_id=1, source_target_pairs={{64,0},{68,4},{72,8},{76,12},{80,16},{84,20},{88,24},{92,28},{96,3... | collective-permute-start | bytes 540680 | tf_op jit(solution)/shard_map/ppermute | solution.py:18
  20.9 6.1 collective-permute-start.1
  26.9 4.9 collective-permute-start.2
  31.9 1.9 collective-permute-start.3
  33.8 16.8 %collective-permute-done.1 = bf16[256,352]{0,1:T(8,128)(2,1)S(1)} collective-permute-done((bf16[256,352]{0,1:T(8,128)(2,1)S(1)}, bf16[256,352]{0,1:T(8,128)(2,1)S(1)}, u32[]{:S(2)}, u32[]{:S(2)}) %collective-permute-start.1) | collective-permute-done | bytes 180256 | tf_op jit(solution)/shard_map/ppermute | solution.py:18
  50.6 3.5 collective-permute-done.2
  54.1 3.1 collective-permute-done.3
  57.2 0.1 maximum_bitcast_fusion
  57.3 1.0 copy.39
  58.3 0.0 all-gather.4.cloned.1.call-update
  58.3 0.0 all-gather.8.cloned.1.call-start
  58.4 0.7 all-gather.8.cloned.1.call-update
  59.1 0.0 all-gather.6.cloned.1.call-start
  59.1 0.3 reshape.70
  59.4 0.2 reduce_window_sum.14
  59.6 0.1 convert_reduce_fusion
  59.7 1.0 compare_select_fusion
  60.7 45.1 %all-gather.4.cloned.1.call-done = bf16[1024,1408]{0,1:T(8,128)(2,1)} async-done(((bf16[1024,352]{0,1:T(8,128)(2,1)}), bf16[1024,1408]{0,1:T(8,128)(2,1)}) %all-gather.4.cloned.1.call-update) | async-done | bytes 2883600 | tf_op jit(solution)/shard_map/all_gather | solution.py:61
  105.7 3.7 convolution_convert_fusion
  109.4 0.9 reshape.69
  110.2 0.4 fusion.48
  110.6 0.5 fusion.36
  111.1 0.1 copy-done.2
  111.2 2.4 fusion.51
  113.6 3.0 fusion.26
  116.6 3.0 fusion.23
  119.6 2.1 fusion.29
  121.6 0.1 pad_maximum_fusion
  121.8 0.6 copy.31
  122.3 1.2 copy.41
  123.6 0.0 all-gather.6.cloned.1.call-update
  123.6 0.0 all-reduce.2.cloned.1.call-start
  123.6 0.9 copy-done.4
  124.5 4.8 fusion.52
  129.3 0.0 all-reduce.2.cloned.1.call-update
  129.4 49.1 %all-gather.8.cloned.1.call-done = bf16[1408,2112]{0,1:T(8,128)(2,1)} async-done(((bf16[1408,528]{0,1:T(8,128)(2,1)}), bf16[1408,2112]{0,1:T(8,128)(2,1)}) %all-gather.8.cloned.1.call-update) | async-done | bytes 5947408 | tf_op jit(solution)/shard_map/all_gather | solution.py:62
  178.5 60.4 %all-gather.6.cloned.1.call-done = bf16[1024,2112]{0,1:T(8,128)(2,1)} async-done(((bf16[1024,528]{0,1:T(8,128)(2,1)}), bf16[1024,2112]{0,1:T(8,128)(2,1)}) %all-gather.6.cloned.1.call-update) | async-done | bytes 4325392 | tf_op jit(solution)/shard_map/all_gather | solution.py:100
  238.9 5.2 fusion.14
  244.1 4.2 collective-permute-start.4
  248.3 10.6 %collective-permute-start.5 = (bf16[256,352]{0,1:T(8,128)(2,1)S(1)}, bf16[256,352]{0,1:T(8,128)(2,1)S(1)}, u32[]{:S(2)}, u32[]{:S(2)}) collective-permute-start(bf16[256,352]{0,1:T(8,128)(2,1)S(1)} %get-tuple-element.10), channel_id=1, source_target_pairs={{320,0},{324,4},{328,8},{332,12},{336,16},{340,20},{344,24},{348,2... | collective-permute-start | bytes 540680 | tf_op jit(solution)/shard_map/ppermute | solution.py:18
  258.9 1.9 collective-permute-start.6
  260.8 2.7 collective-permute-start.7
  263.5 348.4 %all-reduce.2.cloned.1.call-done = f32[1408,528]{0,1:T(8,128)} async-done(((f32[1408,528]{0,1:T(8,128)}), f32[1408,528]{0,1:T(8,128)}) %all-reduce.2.cloned.1.call-update) | async-done | bytes 2973712 | tf_op jit(solution)/shard_map/psum | solution.py:99
  612.0 3.2 multiply_convert_fusion
  615.2 0.1 maximum_bitcast_fusion.1
  615.3 1.0 copy.40
  (16 shorter events, 0.1 us)
Async XLA Ops:
  7.2 98.5 %all-gather.4.cloned.1.call-start = ((), (), s32[]{:S(2)}) async-start(), calls=%async_computation | async-start | bytes 3604480 | tf_op jit(solution)/shard_map/all_gather | solution.py:61
  8.5 25.3 %collective-permute-start = (bf16[256,352]{0,1:T(8,128)(2,1)S(1)}, bf16[256,352]{0,1:T(8,128)(2,1)S(1)}, u32[]{:S(2)}, u32[]{:S(2)}) collective-permute-start(bf16[256,352]{0,1:T(8,128)(2,1)S(1)} %get-tuple-element.11), channel_id=1, source_target_pairs={{64,0},{68,4},{72,8},{76,12},{80,16},{84,20},{88,24},{92,28},{96,3... | collective-permute-start | bytes 540680 | tf_op jit(solution)/shard_map/ppermute | solution.py:18
  20.9 29.8 %collective-permute-start.1 = (bf16[256,352]{0,1:T(8,128)(2,1)S(1)}, bf16[256,352]{0,1:T(8,128)(2,1)S(1)}, u32[]{:S(2)}, u32[]{:S(2)}) collective-permute-start(bf16[256,352]{0,1:T(8,128)(2,1)S(1)} %get-tuple-element.12), channel_id=1, source_target_pairs={{192,0},{196,4},{200,8},{204,12},{208,16},{212,20},{216,24},{220,2... | collective-permute-start | bytes 540680 | tf_op jit(solution)/shard_map/ppermute | solution.py:18
  26.9 27.2 %collective-permute-start.2 = (bf16[256,352]{0,1:T(8,128)(2,1)S(1)}, bf16[256,352]{0,1:T(8,128)(2,1)S(1)}, u32[]{:S(2)}, u32[]{:S(2)}) collective-permute-start(bf16[256,352]{0,1:T(8,128)(2,1)S(1)} %get-tuple-element.14), channel_id=1, source_target_pairs={{320,0},{324,4},{328,8},{332,12},{336,16},{340,20},{344,24},{348,2... | collective-permute-start | bytes 540680 | tf_op jit(solution)/shard_map/ppermute | solution.py:18
  31.9 25.3 %collective-permute-start.3 = (bf16[256,352]{0,1:T(8,128)(2,1)S(1)}, bf16[256,352]{0,1:T(8,128)(2,1)S(1)}, u32[]{:S(2)}, u32[]{:S(2)}) collective-permute-start(bf16[256,352]{0,1:T(8,128)(2,1)S(1)} %get-tuple-element.13), channel_id=1, source_target_pairs={{448,0},{452,4},{456,8},{460,12},{464,16},{468,20},{472,24},{476,2... | collective-permute-start | bytes 540680 | tf_op jit(solution)/shard_map/ppermute | solution.py:18
  57.3 1.8 copy-start.1
  57.3 2.1 copy-start.3
  57.3 48.4 %copy-start = (bf16[1408,528]{0,1:T(8,128)(2,1)S(1)}, bf16[1408,528]{0,1:T(8,128)(2,1)}, u32[]{:S(2)}) copy-start(bf16[1408,528]{0,1:T(8,128)(2,1)} %param.6) | copy-start | bytes 4460548
  58.3 120.2 %all-gather.8.cloned.1.call-start = ((), (), s32[]{:S(2)}) async-start(), calls=%async_computation.2 | async-start | bytes 7434240 | tf_op jit(solution)/shard_map/all_gather | solution.py:62
  59.1 179.8 %all-gather.6.cloned.1.call-start = ((), (), s32[]{:S(2)}) async-start(), calls=%async_computation.1 | async-start | bytes 5406720 | tf_op jit(solution)/shard_map/all_gather | solution.py:100
  110.2 1.0 copy-start.2
  122.3 2.2 copy-start.4
  123.6 488.4 %all-reduce.2.cloned.1.call-start = ((), (), s32[]{:S(2)}) async-start(), calls=%async_computation.3 | async-start | bytes 5947392 | tf_op jit(solution)/shard_map/psum | solution.py:99
  244.1 371.0 %collective-permute-start.4 = (bf16[256,352]{0,1:T(8,128)(2,1)S(1)}, bf16[256,352]{0,1:T(8,128)(2,1)S(1)}, u32[]{:S(2)}, u32[]{:S(2)}) collective-permute-start(bf16[256,352]{0,1:T(8,128)(2,1)S(1)} %get-tuple-element.7), channel_id=1, source_target_pairs={{448,0},{452,4},{456,8},{460,12},{464,16},{468,20},{472,24},{476,2... | collective-permute-start | bytes 540680 | tf_op jit(solution)/shard_map/ppermute | solution.py:18
  248.3 366.9 %collective-permute-start.5 = (bf16[256,352]{0,1:T(8,128)(2,1)S(1)}, bf16[256,352]{0,1:T(8,128)(2,1)S(1)}, u32[]{:S(2)}, u32[]{:S(2)}) collective-permute-start(bf16[256,352]{0,1:T(8,128)(2,1)S(1)} %get-tuple-element.10), channel_id=1, source_target_pairs={{320,0},{324,4},{328,8},{332,12},{336,16},{340,20},{344,24},{348,2... | collective-permute-start | bytes 540680 | tf_op jit(solution)/shard_map/ppermute | solution.py:18
  258.9 356.3 %collective-permute-start.6 = (bf16[256,352]{0,1:T(8,128)(2,1)S(1)}, bf16[256,352]{0,1:T(8,128)(2,1)S(1)}, u32[]{:S(2)}, u32[]{:S(2)}) collective-permute-start(bf16[256,352]{0,1:T(8,128)(2,1)S(1)} %get-tuple-element.9), channel_id=1, source_target_pairs={{192,0},{196,4},{200,8},{204,12},{208,16},{212,20},{216,24},{220,2... | collective-permute-start | bytes 540680 | tf_op jit(solution)/shard_map/ppermute | solution.py:18
  260.8 354.4 %collective-permute-start.7 = (bf16[256,352]{0,1:T(8,128)(2,1)S(1)}, bf16[256,352]{0,1:T(8,128)(2,1)S(1)}, u32[]{:S(2)}, u32[]{:S(2)}) collective-permute-start(bf16[256,352]{0,1:T(8,128)(2,1)S(1)} %get-tuple-element.8), channel_id=1, source_target_pairs={{64,0},{68,4},{72,8},{76,12},{80,16},{84,20},{88,24},{92,28},{96,3... | collective-permute-start | bytes 540680 | tf_op jit(solution)/shard_map/ppermute | solution.py:18
Sparse Core Ops, SparseCore 0:
  58.4 47.2 all-gather.3
  107.8 70.6 all-gather.7
  181.2 57.6 all-gather.5
  242.2 369.7 all-reduce.1
where the time goes:
time: 623 us
  waiting for transfers between devices  527 us (85%)
  starting transfers between devices  44.8 us (7%)
  matrix products  24.6 us (4%)
  between operations  14 us (2%)
  local copies, waits for them, and re-layouts  7.45 us (1%)
    psum x1, waiting for transfers between devices, shards(): lax.psum(weight_term, 'dp') * norm_factor  348 us
    all_gather x1, waiting for transfers between devices, shards(): grad_all = lax.all_gather(grad_packed, 'mp', axis=1, tiled=True)  60.4 us
    all_gather x1, waiting for transfers between devices, shards(): full_weight = lax.all_gather(qkv_weight, 'mp', axis=1, tiled=True)  49.1 us
    all_gather x1, waiting for transfers between devices, shards(): seq_rows = lax.all_gather(local_rows, 'mp', axis=1, tiled=True)  45.1 us
    ppermute x8, starting transfers between devices, from_behind(): return lax.ppermute(block, axis, route)  44.7 us
    ppermute x8, waiting for transfers between devices, from_behind(): return lax.ppermute(block, axis, route)  23.4 us
  transfers between devices with their start and end apart: 12, of which 7 were waited for; matrix products, arithmetic and copies ran while one was open for 5% of the time, Pallas kernels for 0%

commit v1 on v0

v1 whole, which is shorter than its diff:
```python
import functools
import math

import jax
import jax.numpy as jnp
from jax import lax
from jax.experimental import pallas as pl
from jax.experimental.pallas import tpu as pltpu
from jax.sharding import PartitionSpec as P

HD = 88
IMGS = 4
BUNDLES = 4
CAP = 256
SEQ = 1024
YS = 4
XS = 4
CORES = 2
LANES = 128
GROW = 192

F32 = jnp.float32
BF16 = jnp.bfloat16


def dot(a, b, dims):
    return lax.dot_general(a, b, (dims, ((), ())), preferred_element_type=F32)


def routed_rows(counts_here, grad_context):
    ends = jnp.cumsum(counts_here, axis=1)
    position = jnp.arange(CAP, dtype=jnp.int32)
    segment = jnp.sum((position[None, :, None] >= ends[:, None, :]).astype(jnp.int32), axis=2)
    is_valid = segment < IMGS
    ids = jnp.where(is_valid, segment - IMGS, position[None]).astype(BF16)
    heads = grad_context.shape[1] // HD
    up = grad_context.reshape(BUNDLES, CAP, heads, HD) * is_valid[:, :, None, None].astype(BF16)
    up = up.transpose(0, 2, 3, 1)
    tags = jnp.broadcast_to(ids[:, None, None, :], (BUNDLES, heads, 8, CAP))
    return jnp.concatenate([up, tags], axis=2).reshape(BUNDLES, heads * (HD + 8), CAP)


def kernel(
    n_dp,
    x_hbm, g_hbm, w_hbm,
    gx_hbm, fin_hbm,
    xs, big_x, wv, wt, gb, pk, gps, gp, wfb, wf, dw, c0, ra1, ra2, rb1, rb2, ze, zr, fin, gxv,
    x_ss, x_rs, g_ss, g_rs, p_ss, p_rs, w_ss, w_rs, v_ss, v_rs, d_ss, d_rs, z_ss, z_rs, f_ss, f_rs, l_sem, o_sem,
):
    feat = x_hbm.shape[1]
    width = w_hbm.shape[1]
    heads = width // (3 * HD)
    d_model = YS * feat
    nz = n_dp // (XS * CORES)
    stride = n_dp // BUNDLES
    scale = 1.0 / math.sqrt(HD)
    norm = 1.0 / math.sqrt(n_dp)
    half = fin.shape[0] // 2
    sub = half // 2
    q1 = sub // 2
    q2 = q1 // 2
    piece = 2 * q2 // nz

    dp = lax.axis_index("dp")
    me = lax.axis_index("mp")
    right, left, far = (me + 1) % YS, (me + 3) % YS, (me + 2) % YS
    core = dp % CORES
    xi = (dp // CORES) % XS
    zi = dp // (XS * CORES)
    base_xz = zi * (XS * CORES)
    mate = {"dp": dp + 1 - 2 * core}
    even = xi % 2
    near1 = {"dp": base_xz + (xi + 1 - 2 * even) * CORES + core}
    near2 = {"dp": base_xz + ((xi + 3 - 2 * even) % XS) * CORES + core}
    bit1 = ((xi + 1) // 2) % 2
    bit2 = xi // 2

    def z_peer(k):
        return {"dp": ((zi + k) % nz) * (XS * CORES) + xi * CORES + core}

    def remote(src, dst, ss, rs, dev):
        return pltpu.make_async_remote_copy(
            src_ref=src, dst_ref=dst, send_sem=ss, recv_sem=rs,
            device_id=dev, device_id_type=pl.DeviceIdType.MESH,
        )

    def rows(start, size):
        return pl.ds(pl.multiple_of(start, 16), size)

    def order(i):
        return (3 * i) % BUNDLES

    def g_copy(b):
        off = stride // 2 + b * stride
        return remote(g_hbm.at[b], gb.at[b], g_ss.at[b], g_rs.at[b], {"dp": (dp + off) % n_dp})

    def x_copies(b):
        r = rows(b * CAP, CAP)
        return (
            remote(x_hbm.at[r], xs.at[me, r], x_ss.at[0, b], x_rs.at[0, b], {"mp": right}),
            remote(x_hbm.at[r], xs.at[me, r], x_ss.at[1, b], x_rs.at[1, b], {"mp": left}),
        )

    def x_relays(b):
        r = rows(b * CAP, CAP // 2)
        s = rows(b * CAP + CAP // 2, CAP // 2)
        return (
            remote(xs.at[left, r], xs.at[left, r], x_ss.at[2, b], x_rs.at[2, b], {"mp": right}),
            remote(xs.at[right, s], xs.at[right, s], x_ss.at[3, b], x_rs.at[3, b], {"mp": left}),
        )

    def p_copies(b):
        r = rows(me * width, width)
        return (
            remote(gp.at[b, r], gp.at[b, r], p_ss.at[0, b], p_rs.at[0, b], {"mp": right}),
            remote(gp.at[b, r], gp.at[b, r], p_ss.at[1, b], p_rs.at[1, b], {"mp": left}),
        )

    def p_relays(b):
        r = rows(left * width, 256)
        s = rows(right * width + 256, width - 256)
        return (
            remote(gp.at[b, r], gp.at[b, r], p_ss.at[2, b], p_rs.at[2, b], {"mp": right}),
            remote(gp.at[b, s], gp.at[b, s], p_ss.at[3, b], p_rs.at[3, b], {"mp": left}),
        )

    fh = feat // CORES

    def w_copy(k):
        to = (me + k) % YS
        return remote(
            w_hbm.at[rows(to * feat + core * fh, fh)], wfb.at[me, rows(core * fh, fh)],
            w_ss.at[k - 1], w_rs.at[k - 1], {"mp": to},
        )

    def v_copy(k):
        who = (me + YS - k) % YS
        r = rows(core * fh, fh)
        return remote(wfb.at[who, r], wfb.at[who, r], v_ss.at[k - 1], v_rs.at[k - 1], mate)

    own = core * half
    oa, ob = own, own + sub
    keep_a, keep_b = oa + bit1 * q1, ob + bit2 * q1
    fa, fb = keep_a + bit2 * q2, keep_b + bit1 * q2
    core_rs = remote(dw.at[rows((1 - core) * half, half)], c0, d_ss.at[0], d_rs.at[0], mate)
    a1 = remote(dw.at[rows(oa + (1 - bit1) * q1, q1)], ra1, d_ss.at[1], d_rs.at[1], near1)
    b1 = remote(dw.at[rows(ob + (1 - bit2) * q1, q1)], rb1, d_ss.at[2], d_rs.at[2], near2)
    give_a2, give_b2 = keep_a + (1 - bit2) * q2, keep_b + (1 - bit1) * q2
    a2 = remote(dw.at[rows(give_a2, q2)], ra2, d_ss.at[3], d_rs.at[3], near2)
    b2 = remote(dw.at[rows(give_b2, q2)], rb2, d_ss.at[4], d_rs.at[4], near1)

    def z_copy(k):
        to = (zi + k) % nz
        return remote(ze.at[rows(to * piece, piece)], zr.at[k], z_ss.at[k], z_rs.at[k], z_peer(k))

    def spot(z):
        return jnp.where(z < nz // 2, fa + z * piece, fb + (z - nz // 2) * piece)

    def f_copy(k):
        r = rows(spot(zi), piece)
        return remote(fin.at[r], fin.at[r], f_ss.at[k], f_rs.at[k], z_peer(k))

    def same(start, size, i, dev):
        r = rows(start, size)
        return remote(fin.at[r], fin.at[r], d_ss.at[i], d_rs.at[i], dev)

    ag_a2, ag_b2 = same(fa, q2, 5, near2), same(fb, q2, 6, near1)
    ag_a1, ag_b1 = same(keep_a, q1, 7, near1), same(keep_b, q1, 8, near2)
    ag_core = same(own, half, 9, mate)

    barrier = pltpu.get_barrier_semaphore()
    mesh_id = pl.DeviceIdType.MESH
    for dev in [{"mp": right}, {"mp": left}, {"mp": far}, mate, near1, near2]:
        pl.semaphore_signal(barrier, inc=1, device_id=dev, device_id_type=mesh_id)

    def greet(k, _):
        pl.semaphore_signal(barrier, inc=1, device_id=z_peer(k), device_id_type=mesh_id)
        return 0

    lax.fori_loop(1, nz, greet, 0)
    pl.semaphore_wait(barrier, 6 + nz - 1)

    def start(copies):
        for cp in copies:
            cp.start()

    def arrive(copies):
        for cp in copies:
            cp.wait_recv()

    start(x_copies(0))
    for i in range(BUNDLES):
        g_copy(order(i)).start()
    start(x_copies(order(1)))
    w_local = pltpu.make_async_copy(w_hbm, wv, l_sem.at[0])
    w_local.start()
    x_local = pltpu.make_async_copy(x_hbm, xs.at[me], l_sem.at[1])
    x_local.start()
    wf_local = pltpu.make_async_copy(w_hbm.at[rows(me * feat, feat)], wfb.at[me], l_sem.at[2])
    wf_local.start()

    big_x[:, d_model:] = jnp.zeros((SEQ, big_x.shape[1] - d_model), BF16)
    w_local.wait()
    for n in range(d_model // LANES):
        wt[:, n * LANES:(n + 1) * LANES] = wv[n * LANES:(n + 1) * LANES, :].T
    x_local.wait()

    arrive(x_copies(0))
    start(x_relays(0))
    start(x_copies(order(2)))

    def bundle(i, _):
        b = order(i)

        @pl.when(i < BUNDLES - 1)
        def _():
            nxt = order(i + 1)
            arrive(x_copies(nxt))
            start(x_relays(nxt))

        @pl.when(i == 0)
        def _():
            start(x_copies(order(3)))

        @pl.when(i == 2)
        def _():
            for k in range(1, YS):
                w_copy(k).start()
            start(p_copies(order(0)))
            start(p_copies(order(1)))

        @pl.when(i == 3)
        def _():
            start(p_copies(order(2)))

        arrive(x_relays(b))
        r = rows(b * CAP, CAP)
        for j in range(YS):
            big_x[r, j * feat:(j + 1) * feat] = xs[j, r, :]
        pk[...] = dot(wt[...], big_x[r, :d_model], ((1,), (1,)))
        g_copy(b).wait_recv()
        tags = gb[b, GROW // 2 - 16:GROW // 2, :].astype(F32)[8:16]
        allowed = tags[0:1, :] == tags.T[:, 0:1]
        for h in range(heads):
            o = h * 3 * HD
            query = pk[o:o + HD, :].astype(BF16)
            key = pk[o + HD:o + 2 * HD, :].astype(BF16)
            value = pk[o + 2 * HD:o + 3 * HD, :].astype(BF16)
            up = gb[b, h * (HD + 8):h * (HD + 8) + HD, :]
            scores = dot(query, key, ((0,), (0,))) * scale
            masked = jnp.where(allowed, scores, -1e30)
            top = jnp.max(masked, axis=1, keepdims=True)
            exponent = jnp.where(allowed, jnp.exp(masked - top), 0.0)
            probs = exponent * (1.0 / jnp.sum(exponent, axis=1, keepdims=True))
            grad_probs = dot(up, value, ((0,), (0,)))
            row_dot = jnp.sum(probs * grad_probs, axis=1, keepdims=True)
            logits = (probs * (grad_probs - row_dot) * scale).astype(BF16)
            gps[o:o + HD, :] = dot(key, logits, ((1,), (1,)))
            gps[o + HD:o + 2 * HD, :] = dot(query, logits, ((1,), (0,)))
            gps[o + 2 * HD:o + 3 * HD, :] = dot(up, probs.astype(BF16), ((1,), (0,)))
        gp[b, rows(me * width, width), :] = gps[...].astype(BF16)
        return 0

    lax.fori_loop(0, BUNDLES, bundle, 0)
    start(p_copies(order(3)))

    mine = rows(me * width, width)

    def weight_block(n, _):
        cols = pl.ds(pl.multiple_of(n * 2 * LANES, 2 * LANES), 2 * LANES)
        total = dot(gp[0, mine, :], big_x[0:CAP, cols], ((1,), (0,)))
        for b in range(1, BUNDLES):
            total += dot(gp[b, mine, :], big_x[b * CAP:(b + 1) * CAP, cols], ((1,), (0,)))
        at = n * 2 * width
        dw[rows(at, width), :] = total[:, :LANES]
        dw[rows(at + width, width), :] = total[:, LANES:]
        return 0

    lax.fori_loop(0, big_x.shape[1] // (2 * LANES), weight_block, 0)
    core_rs.start()

    for k in range(1, YS):
        w_copy(k).wait_recv()
        v_copy(k).start()
    core_rs.wait_recv()

    def add_core(n, _):
        r = rows(own + n * q2, q2)
        dw[r, :] += c0[rows(n * q2, q2), :]
        return 0

    lax.fori_loop(0, half // q2, add_core, 0)
    a1.start()
    b1.start()

    wf_local.wait()
    for k in range(1, YS):
        v_copy(k).wait_recv()
    for j in range(YS):
        wf[:, j * width:(j + 1) * width] = wfb[j]

    a1.wait_recv()
    b1.wait_recv()

    def add_into(at, got, got_at, size):
        dw[rows(at, size), :] += got[rows(got_at, size), :]

    add_into(give_a2, ra1, (1 - bit2) * q2, q2)
    add_into(give_b2, rb1, (1 - bit1) * q2, q2)
    a2.start()
    b2.start()
    add_into(fa, ra1, bit2 * q2, q2)
    add_into(fb, rb1, bit1 * q2, q2)

    for i in range(2):
        arrive(p_copies(order(i)))
        start(p_relays(order(i)))

    a2.wait_recv()
    b2.wait_recv()
    ze[0:q2, :] = dw[rows(fa, q2), :] + ra2[...]
    ze[q2:2 * q2, :] = dw[rows(fb, q2), :] + rb2[...]

    def loop_z(f):
        def body(k, _):
            f(k)
            return 0

        lax.fori_loop(1, nz, body, 0)

    loop_z(lambda k: z_copy(k).start())

    for i in range(2, BUNDLES):
        arrive(p_copies(order(i)))
        start(p_relays(order(i)))

    def gx_copy(b):
        return pltpu.make_async_copy(gxv.at[b], gx_hbm.at[b], o_sem.at[b])

    def rows_grad(i, _):
        b = order(i)
        arrive(p_relays(b))
        gxv[b] = dot(wf[...], gp[b], ((1,), (0,))).astype(BF16)
        gx_copy(b).start()
        return 0

    lax.fori_loop(0, BUNDLES, rows_grad, 0)

    loop_z(lambda k: z_copy(k).wait_recv())

    def add_z(k, total):
        return total + zr[k]

    total = lax.fori_loop(1, nz, add_z, ze[rows(zi * piece, piece), :])
    fin[rows(spot(zi), piece), :] = (total * norm).astype(BF16)
    loop_z(lambda k: f_copy(k).start())
    loop_z(lambda k: f_copy(k).wait_recv())
    ag_a2.start()
    ag_b2.start()
    ag_a2.wait_recv()
    ag_b2.wait_recv()
    ag_a1.start()
    ag_b1.start()
    ag_a1.wait_recv()
    ag_b1.wait_recv()
    ag_core.start()
    mine_out = pltpu.make_async_copy(
        fin.at[rows(own, half)], fin_hbm.at[rows(own, half)], o_sem.at[BUNDLES])
    mine_out.start()
    ag_core.wait_recv()
    rest_out = pltpu.make_async_copy(
        fin.at[rows((1 - core) * half, half)], fin_hbm.at[rows((1 - core) * half, half)],
        o_sem.at[BUNDLES + 1])
    rest_out.start()

    for b in range(BUNDLES):
        g_copy(b).wait_send()
        for cp in x_copies(b) + x_relays(b) + p_copies(b) + p_relays(b):
            cp.wait_send()
        gx_copy(b).wait()
    for k in range(1, YS):
        w_copy(k).wait_send()
        v_copy(k).wait_send()
    for cp in (core_rs, a1, b1, a2, b2, ag_a2, ag_b2, ag_a1, ag_b1, ag_core):
        cp.wait_send()
    loop_z(lambda k: z_copy(k).wait_send())
    loop_z(lambda k: f_copy(k).wait_send())
    mine_out.wait()
    rest_out.wait()


def shards(patches, counts, qkv_weight, grad_context):
    n_dp = lax.axis_size("dp")
    nz = n_dp // (XS * CORES)
    feat = patches.shape[1]
    width = qkv_weight.shape[1]
    d_model = YS * feat
    blocks = d_model // LANES
    parts = n_dp
    unit = -(-(blocks * width) // (parts * 16)) * 16
    flat = unit * parts
    wide = 2 * LANES * (-(-blocks // 2))
    half = flat // 2
    q1, q2 = half // 4, half // 8
    routed = routed_rows(counts[0], grad_context)
    dma = pltpu.SemaphoreType.DMA
    any_spec = pl.BlockSpec(memory_space=pl.ANY)
    gx, fin = pl.pallas_call(
        functools.partial(kernel, n_dp),
        out_shape=(
            jax.ShapeDtypeStruct((BUNDLES, feat, CAP), BF16),
            jax.ShapeDtypeStruct((flat, LANES), BF16),
        ),
        in_specs=[any_spec] * 3,
        out_specs=(any_spec, any_spec),
        scratch_shapes=[
            pltpu.VMEM((YS, SEQ, feat), BF16),
            pltpu.VMEM((SEQ, wide), BF16),
            pltpu.VMEM((d_model, width), BF16),
            pltpu.VMEM((width, d_model), BF16),
            pltpu.VMEM((BUNDLES, GROW, CAP), BF16),
            pltpu.VMEM((width, CAP), F32),
            pltpu.VMEM((width, CAP), F32),
            pltpu.VMEM((BUNDLES, YS * width, CAP), BF16),
            pltpu.VMEM((YS, feat, width), BF16),
            pltpu.VMEM((feat, YS * width), BF16),
            pltpu.VMEM((max(flat, wide // LANES * width), LANES), F32),
            pltpu.VMEM((half, LANES), F32),
            pltpu.VMEM((q1, LANES), F32),
            pltpu.VMEM((q2, LANES), F32),
            pltpu.VMEM((q1, LANES), F32),
            pltpu.VMEM((q2, LANES), F32),
            pltpu.VMEM((2 * q2, LANES), F32),
            pltpu.VMEM((nz, 2 * q2 // nz, LANES), F32),
            pltpu.VMEM((flat, LANES), BF16),
            pltpu.VMEM((BUNDLES, feat, CAP), BF16),
            dma((4, BUNDLES)), dma((4, BUNDLES)),
            dma((BUNDLES,)), dma((BUNDLES,)),
            dma((4, BUNDLES)), dma((4, BUNDLES)),
            dma((YS - 1,)), dma((YS - 1,)),
            dma((YS - 1,)), dma((YS - 1,)),
            dma((10,)), dma((10,)),
            dma((nz,)), dma((nz,)),
            dma((nz,)), dma((nz,)),
            dma((3,)), dma((BUNDLES + 2,)),
        ],
        compiler_params=pltpu.CompilerParams(
            collective_id=0, has_side_effects=True, vmem_limit_bytes=60 * 1024 * 1024),
        name="layer",
    )(patches, routed, qkv_weight)
    grad_patches = gx.transpose(0, 2, 1).reshape(SEQ, feat)
    grad_weight = fin[:blocks * width].reshape(blocks, width, LANES).transpose(0, 2, 1)
    return grad_patches, grad_weight.reshape(d_model, width)


def solution(mesh):
    in_specs = (P("dp", "mp"), P("dp", None, None), P(None, "mp"), P("dp", "mp"))
    out_specs = (P("dp", "mp"), P(None, "mp"))
    return jax.shard_map(shards, mesh=mesh, in_specs=in_specs, out_specs=out_specs, check_vma=False)
```

time: 623 us -> 132 us (0.21)
  waiting for transfers between devices: 527 us -> 0 us
  Pallas kernels: 0 us -> 117 us
  starting transfers between devices: 44.8 us -> 0 us
  matrix products: 24.6 us -> 0 us
  between operations: 14 us -> 0.7 us
    psum x1 -> x0, waiting for transfers between devices: 348 us -> none  [shards(): lax.psum(weight_term, 'dp') * norm_factor]
    all_gather x3 -> x0, waiting for transfers between devices: 155 us -> none  [the longest x1 60.4 us: shards(): grad_all = lax.all_gather(grad_packed, 'mp', axis=1, tiled=True)]
    pallas_call x0 -> x1, Pallas kernels: none -> 117 us  [shards(): pl.pallas_call(functools.partial(kernel, n_dp), out_shape=(jax.ShapeDtype...]
    ppermute x8 -> x0, starting transfers between devices: 44.7 us -> none  [from_behind(): return lax.ppermute(block, axis, route)]
    ppermute x8 -> x0, waiting for transfers between devices: 23.4 us -> none  [from_behind(): return lax.ppermute(block, axis, route)]
    dot_general x7 -> x0, matrix products: 22.2 us -> none  [the longest x1 5.19 us: shards(): lax.dot_general(grad_all, weight_here, (((1,), (1,)), ((), ())), preferre...]
  transfers between devices with their start and end apart: 12 -> 0, of which waited for: 7 -> 0; matrix products, arithmetic and copies ran while one was open for 5% -> 0% of each run, Pallas kernels for 0% -> 0%
where the time goes in v1:
time: 132 us
  Pallas kernels  117 us (89%)
  local copies, waits for them, and re-layouts  12.1 us (9%)
  other arithmetic  1.85 us (1%)
    pallas_call x1, Pallas kernels, shards(): pl.pallas_call(functools.partial(kernel, n_dp), out_shape=(jax.ShapeDtype...  117 us
    unnamed x7, local copies, waits for them, and re-layouts  5.58 us

profile of v1, /device:TPU:1, one launch (start us, length us, event | category | flops | bytes accessed | tf_op | source)
XLA Modules:
  0.0 131.8 jit_solution(4973470995062594197)
XLA Ops:
  0.6 0.0 copy-start.1
  0.6 0.9 reduce_window_sum.14
  1.6 0.1 convert_reduce_fusion
  1.7 1.3 reshape.39
  2.9 0.0 copy-start
  3.0 0.1 fusion
  3.0 0.8 pad_maximum_fusion
  3.8 0.0 copy-done.1
  3.8 1.2 copy.17.x_hbm
  4.9 0.0 copy-done
  5.0 2.2 %copy.18.w_hbm = bf16[1408,528]{1,0:T(8,128)(2,1)} copy(bf16[1408,528]{0,1:T(8,128)(2,1)S(1)} %copy-done) | data formatting | bytes 2973696 | tf_op args[2]
  7.2 117.1 %layer.1 = (bf16[4,352,256]{2,1,0:T(8,128)(2,1)}, bf16[6144,128]{1,0:T(8,128)(2,1)}) custom-call(bf16[1024,352]{1,0:T(8,128)(2,1)} %copy.17.x_hbm, bf16[4,192,256]{2,1,0:T(8,128)(2,1)} %bitcast.15, bf16[1408,528]{1,0:T(8,128)(2,1)} %copy.18.w_hbm), custom_call_target="tpu_custom_call" | custom-call | tf_op jit(solution)/shard_map/layer/pallas_call | solution.py:408
  124.3 2.1 %copy.22 = bf16[4,44,8,256]{3,2,0,1:T(8,128)(2,1)} copy(bf16[4,44,8,256]{3,2,1,0:T(8,128)(2,1)} %bitcast.17) | data formatting | bytes 1441792 | tf_op jit(solution)/shard_map/reshape | solution.py:451
  126.4 1.5 %slice.3 = bf16[5808,128]{1,0:T(8,128)(2,1)S(1)} slice(bf16[6144,128]{1,0:T(8,128)(2,1)} %get-tuple-element.5), slice={[0:5808], [0:128]} | slice | bytes 2973696 | tf_op jit(solution)/shard_map/slice | solution.py:452
  127.9 1.8 %copy.20 = bf16[11,528,128]{1,2,0:T(8,128)(2,1)S(1)} copy(bf16[11,528,128]{2,1,0:T(8,128)(2,1)S(1)} %bitcast.14) | data formatting | bytes 2973696 | tf_op jit(solution)/shard_map/reshape | solution.py:452
  129.6 2.2 %copy.21 = bf16[1408,528]{0,1:T(8,128)(2,1)} copy(bf16[1408,528]{1,0:T(8,128)(2,1)S(1)} %bitcast.13) | data formatting | bytes 2973696
  (3 shorter events, 0.0 us)
Async XLA Ops:
  0.6 3.2 %copy-start.1 = (bf16[1024,352]{0,1:T(8,128)(2,1)S(1)}, bf16[1024,352]{0,1:T(8,128)(2,1)}, u32[]{:S(2)}) copy-start(bf16[1024,352]{0,1:T(8,128)(2,1)} %param.4) | copy-start | bytes 2162692
  2.9 2.0 %copy-start = (bf16[1408,528]{0,1:T(8,128)(2,1)S(1)}, bf16[1408,528]{0,1:T(8,128)(2,1)}, u32[]{:S(2)}) copy-start(bf16[1408,528]{0,1:T(8,128)(2,1)} %param.6) | copy-start | bytes 4460548

commit v2 on v1

--- a/solution.py
+++ b/solution.py
@@ -17,7 +17,7 @@
 XS = 4
 CORES = 2
 LANES = 128
-GROW = 192
+TAG = 16
 
 F32 = jnp.float32
 BF16 = jnp.bfloat16
@@ -27,28 +27,15 @@
     return lax.dot_general(a, b, (dims, ((), ())), preferred_element_type=F32)
 
 
-def routed_rows(counts_here, grad_context):
-    ends = jnp.cumsum(counts_here, axis=1)
-    position = jnp.arange(CAP, dtype=jnp.int32)
-    segment = jnp.sum((position[None, :, None] >= ends[:, None, :]).astype(jnp.int32), axis=2)
-    is_valid = segment < IMGS
-    ids = jnp.where(is_valid, segment - IMGS, position[None]).astype(BF16)
-    heads = grad_context.shape[1] // HD
-    up = grad_context.reshape(BUNDLES, CAP, heads, HD) * is_valid[:, :, None, None].astype(BF16)
-    up = up.transpose(0, 2, 3, 1)
-    tags = jnp.broadcast_to(ids[:, None, None, :], (BUNDLES, heads, 8, CAP))
-    return jnp.concatenate([up, tags], axis=2).reshape(BUNDLES, heads * (HD + 8), CAP)
-
-
 def kernel(
     n_dp,
-    x_hbm, g_hbm, w_hbm,
+    x_hbm, g_hbm, w_hbm, counts,
     gx_hbm, fin_hbm,
-    xs, big_x, wv, wt, gb, pk, gps, gp, wfb, wf, dw, c0, ra1, ra2, rb1, rb2, ze, zr, fin, gxv,
-    x_ss, x_rs, g_ss, g_rs, p_ss, p_rs, w_ss, w_rs, v_ss, v_rs, d_ss, d_rs, z_ss, z_rs, f_ss, f_rs, l_sem, o_sem,
+    xt, wt, wn, tag, gt, gb, pk, up_all, gps, gp, wfb, wf, dw, c0, ra1, ra2, rb1, rb2, ze, zr, fin, gxv,
+    x_ss, x_rs, g_ss, g_rs, t_ss, t_rs, p_ss, p_rs, w_ss, w_rs, v_ss, v_rs, d_ss, d_rs, z_ss, z_rs, f_ss, f_rs, l_sem, o_sem,
 ):
-    feat = x_hbm.shape[1]
-    width = w_hbm.shape[1]
+    feat = x_hbm.shape[0]
+    width = w_hbm.shape[0]
     heads = width // (3 * HD)
     d_model = YS * feat
     nz = n_dp // (XS * CORES)
@@ -90,24 +77,36 @@
     def order(i):
         return (3 * i) % BUNDLES
 
+    def cols(b):
+        return pl.ds(pl.multiple_of(b * CAP, CAP), CAP)
+
     def g_copy(b):
         off = stride // 2 + b * stride
-        return remote(g_hbm.at[b], gb.at[b], g_ss.at[b], g_rs.at[b], {"dp": (dp + off) % n_dp})
+        to = {"dp": (dp + off) % n_dp}
+        return (
+            remote(tag.at[b], gt.at[b], t_ss.at[b], t_rs.at[b], to),
+            remote(g_hbm.at[:, cols(b)], gb.at[b], g_ss.at[b], g_rs.at[b], to),
+        )
 
     def x_copies(b):
-        r = rows(b * CAP, CAP)
+        src = x_hbm.at[:, cols(b)]
+        r = rows(me * feat, feat)
         return (
-            remote(x_hbm.at[r], xs.at[me, r], x_ss.at[0, b], x_rs.at[0, b], {"mp": right}),
-            remote(x_hbm.at[r], xs.at[me, r], x_ss.at[1, b], x_rs.at[1, b], {"mp": left}),
+            remote(src, xt.at[b, r], x_ss.at[0, b], x_rs.at[0, b], {"mp": right}),
+            remote(src, xt.at[b, r], x_ss.at[1, b], x_rs.at[1, b], {"mp": left}),
         )
 
     def x_relays(b):
-        r = rows(b * CAP, CAP // 2)
-        s = rows(b * CAP + CAP // 2, CAP // 2)
+        r = rows(left * feat, feat // 2)
+        s = rows(right * feat + feat // 2, feat // 2)
         return (
-            remote(xs.at[left, r], xs.at[left, r], x_ss.at[2, b], x_rs.at[2, b], {"mp": right}),
-            remote(xs.at[right, s], xs.at[right, s], x_ss.at[3, b], x_rs.at[3, b], {"mp": left}),
-        )
+            remote(xt.at[b, r], xt.at[b, r], x_ss.at[2, b], x_rs.at[2, b], {"mp": right}),
+            remote(xt.at[b, s], xt.at[b, s], x_ss.at[3, b], x_rs.at[3, b], {"mp": left}),
+        )
+
+    def x_local(b):
+        return pltpu.make_async_copy(
+            x_hbm.at[:, cols(b)], xt.at[b, rows(me * feat, feat)], l_sem.at[b])
 
     def p_copies(b):
         r = rows(me * width, width)
@@ -129,7 +128,7 @@
     def w_copy(k):
         to = (me + k) % YS
         return remote(
-            w_hbm.at[rows(to * feat + core * fh, fh)], wfb.at[me, rows(core * fh, fh)],
+            wn.at[rows(to * feat + core * fh, fh)], wfb.at[me, rows(core * fh, fh)],
             w_ss.at[k - 1], w_rs.at[k - 1], {"mp": to},
         )
 
@@ -170,14 +169,29 @@
 
     barrier = pltpu.get_barrier_semaphore()
     mesh_id = pl.DeviceIdType.MESH
-    for dev in [{"mp": right}, {"mp": left}, {"mp": far}, mate, near1, near2]:
-        pl.semaphore_signal(barrier, inc=1, device_id=dev, device_id_type=mesh_id)
 
     def greet(k, _):
         pl.semaphore_signal(barrier, inc=1, device_id=z_peer(k), device_id_type=mesh_id)
         return 0
 
     lax.fori_loop(1, nz, greet, 0)
+    for dev in [{"mp": right}, {"mp": left}, {"mp": far}, mate, near1, near2]:
+        pl.semaphore_signal(barrier, inc=1, device_id=dev, device_id_type=mesh_id)
+    w_local = pltpu.make_async_copy(w_hbm, wt, l_sem.at[BUNDLES])
+    w_local.start()
+    for i in range(BUNDLES):
+        x_local(order(i)).start()
+
+    slot = lax.broadcasted_iota(jnp.int32, (TAG, CAP), 1)
+    for b in range(BUNDLES):
+        end = counts[b, 0]
+        ids = jnp.where(slot >= end, 1, 0)
+        for i in range(1, IMGS):
+            end = end + counts[b, i]
+            ids = ids + jnp.where(slot >= end, 1, 0)
+        tag[b] = jnp.where(slot < end, ids - IMGS, slot).astype(F32).astype(BF16)
+    for b in range(BUNDLES):
+        xt[b, d_model:, :] = jnp.zeros((xt.shape[1] - d_model, CAP), BF16)
     pl.semaphore_wait(barrier, 6 + nz - 1)
 
     def start(copies):
@@ -190,20 +204,14 @@
 
     start(x_copies(0))
     for i in range(BUNDLES):
-        g_copy(order(i)).start()
+        start(g_copy(order(i)))
     start(x_copies(order(1)))
-    w_local = pltpu.make_async_copy(w_hbm, wv, l_sem.at[0])
-    w_local.start()
-    x_local = pltpu.make_async_copy(x_hbm, xs.at[me], l_sem.at[1])
-    x_local.start()
-    wf_local = pltpu.make_async_copy(w_hbm.at[rows(me * feat, feat)], wfb.at[me], l_sem.at[2])
-    wf_local.start()
-
-    big_x[:, d_model:] = jnp.zeros((SEQ, big_x.shape[1] - d_model), BF16)
     w_local.wait()
     for n in range(d_model // LANES):
-        wt[:, n * LANES:(n + 1) * LANES] = wv[n * LANES:(n + 1) * LANES, :].T
-    x_local.wait()
+        wn[n * LANES:(n + 1) * LANES, :] = wt[:, n * LANES:(n + 1) * LANES].T
+    for i in range(BUNDLES):
+        x_local(order(i)).wait()
+    wfb[me] = wn[rows(me * feat, feat), :]
 
     arrive(x_copies(0))
     start(x_relays(0))
@@ -234,19 +242,17 @@
             start(p_copies(order(2)))
 
         arrive(x_relays(b))
-        r = rows(b * CAP, CAP)
-        for j in range(YS):
-            big_x[r, j * feat:(j + 1) * feat] = xs[j, r, :]
-        pk[...] = dot(wt[...], big_x[r, :d_model], ((1,), (1,)))
-        g_copy(b).wait_recv()
-        tags = gb[b, GROW // 2 - 16:GROW // 2, :].astype(F32)[8:16]
+        pk[...] = dot(wt[...], xt[b, 0:d_model, :], ((1,), (0,)))
+        arrive(g_copy(b))
+        tags = gt[b].astype(F32)[0:8]
         allowed = tags[0:1, :] == tags.T[:, 0:1]
+        up_all[...] = jnp.where(tags[0:1, :] < 0, gb[b].astype(F32), 0.0)
         for h in range(heads):
             o = h * 3 * HD
             query = pk[o:o + HD, :].astype(BF16)
             key = pk[o + HD:o + 2 * HD, :].astype(BF16)
             value = pk[o + 2 * HD:o + 3 * HD, :].astype(BF16)
-            up = gb[b, h * (HD + 8):h * (HD + 8) + HD, :]
+            up = up_all[h * HD:(h + 1) * HD, :].astype(BF16)
             scores = dot(query, key, ((0,), (0,))) * scale
             masked = jnp.where(allowed, scores, -1e30)
             top = jnp.max(masked, axis=1, keepdims=True)
@@ -267,16 +273,16 @@
     mine = rows(me * width, width)
 
     def weight_block(n, _):
-        cols = pl.ds(pl.multiple_of(n * 2 * LANES, 2 * LANES), 2 * LANES)
-        total = dot(gp[0, mine, :], big_x[0:CAP, cols], ((1,), (0,)))
+        block = rows(n * 2 * LANES, 2 * LANES)
+        total = dot(gp[0, mine, :], xt[0, block, :], ((1,), (1,)))
         for b in range(1, BUNDLES):
-            total += dot(gp[b, mine, :], big_x[b * CAP:(b + 1) * CAP, cols], ((1,), (0,)))
+            total += dot(gp[b, mine, :], xt[b, block, :], ((1,), (1,)))
         at = n * 2 * width
         dw[rows(at, width), :] = total[:, :LANES]
         dw[rows(at + width, width), :] = total[:, LANES:]
         return 0
 
-    lax.fori_loop(0, big_x.shape[1] // (2 * LANES), weight_block, 0)
+    lax.fori_loop(0, xt.shape[1] // (2 * LANES), weight_block, 0)
     core_rs.start()
 
     for k in range(1, YS):
@@ -293,7 +299,6 @@
     a1.start()
     b1.start()
 
-    wf_local.wait()
     for k in range(1, YS):
         v_copy(k).wait_recv()
     for j in range(YS):
@@ -335,7 +340,7 @@
         start(p_relays(order(i)))
 
     def gx_copy(b):
-        return pltpu.make_async_copy(gxv.at[b], gx_hbm.at[b], o_sem.at[b])
+        return pltpu.make_async_copy(gxv.at[b], gx_hbm.at[:, cols(b)], o_sem.at[b])
 
     def rows_grad(i, _):
         b = order(i)
@@ -364,18 +369,18 @@
     ag_a1.wait_recv()
     ag_b1.wait_recv()
     ag_core.start()
-    mine_out = pltpu.make_async_copy(
-        fin.at[rows(own, half)], fin_hbm.at[rows(own, half)], o_sem.at[BUNDLES])
-    mine_out.start()
+
+    def fin_out(n):
+        return pltpu.make_async_copy(
+            fin.at[n * width:(n + 1) * width], fin_hbm.at[:, n * LANES:(n + 1) * LANES],
+            o_sem.at[BUNDLES + n])
+
     ag_core.wait_recv()
-    rest_out = pltpu.make_async_copy(
-        fin.at[rows((1 - core) * half, half)], fin_hbm.at[rows((1 - core) * half, half)],
-        o_sem.at[BUNDLES + 1])
-    rest_out.start()
+    for n in range(d_model // LANES):
+        fin_out(n).start()
 
     for b in range(BUNDLES):
-        g_copy(b).wait_send()
-        for cp in x_copies(b) + x_relays(b) + p_copies(b) + p_relays(b):
+        for cp in g_copy(b) + x_copies(b) + x_relays(b) + p_copies(b) + p_relays(b):
             cp.wait_send()
         gx_copy(b).wait()
     for k in range(1, YS):
@@ -385,15 +390,14 @@
         cp.wait_send()
     loop_z(lambda k: z_copy(k).wait_send())
     loop_z(lambda k: f_copy(k).wait_send())
-    mine_out.wait()
-    rest_out.wait()
+    for n in range(d_model // LANES):
+        fin_out(n).wait()
 
 
 def shards(patches, counts, qkv_weight, grad_context):
     n_dp = lax.axis_size("dp")
     nz = n_dp // (XS * CORES)
-    feat = patches.shape[1]
-    width = qkv_weight.shape[1]
+    feat, width, grads = patches.shape[1], qkv_weight.shape[1], grad_context.shape[1]
     d_model = YS * feat
     blocks = d_model // LANES
     parts = n_dp
@@ -402,24 +406,25 @@
     wide = 2 * LANES * (-(-blocks // 2))
     half = flat // 2
     q1, q2 = half // 4, half // 8
-    routed = routed_rows(counts[0], grad_context)
     dma = pltpu.SemaphoreType.DMA
     any_spec = pl.BlockSpec(memory_space=pl.ANY)
     gx, fin = pl.pallas_call(
         functools.partial(kernel, n_dp),
         out_shape=(
-            jax.ShapeDtypeStruct((BUNDLES, feat, CAP), BF16),
-            jax.ShapeDtypeStruct((flat, LANES), BF16),
+            jax.ShapeDtypeStruct((feat, SEQ), BF16),
+            jax.ShapeDtypeStruct((width, d_model), BF16),
         ),
-        in_specs=[any_spec] * 3,
+        in_specs=[any_spec] * 3 + [pl.BlockSpec(memory_space=pltpu.SMEM)],
         out_specs=(any_spec, any_spec),
         scratch_shapes=[
-            pltpu.VMEM((YS, SEQ, feat), BF16),
-            pltpu.VMEM((SEQ, wide), BF16),
+            pltpu.VMEM((BUNDLES, wide, CAP), BF16),
+            pltpu.VMEM((width, d_model), BF16),
             pltpu.VMEM((d_model, width), BF16),
-            pltpu.VMEM((width, d_model), BF16),
-            pltpu.VMEM((BUNDLES, GROW, CAP), BF16),
+            pltpu.VMEM((BUNDLES, TAG, CAP), BF16),
+            pltpu.VMEM((BUNDLES, TAG, CAP), BF16),
+            pltpu.VMEM((BUNDLES, grads, CAP), BF16),
             pltpu.VMEM((width, CAP), F32),
+            pltpu.VMEM((grads, CAP), F32),
             pltpu.VMEM((width, CAP), F32),
             pltpu.VMEM((BUNDLES, YS * width, CAP), BF16),
             pltpu.VMEM((YS, feat, width), BF16),
@@ -436,21 +441,20 @@
             pltpu.VMEM((BUNDLES, feat, CAP), BF16),
             dma((4, BUNDLES)), dma((4, BUNDLES)),
             dma((BUNDLES,)), dma((BUNDLES,)),
+            dma((BUNDLES,)), dma((BUNDLES,)),
             dma((4, BUNDLES)), dma((4, BUNDLES)),
             dma((YS - 1,)), dma((YS - 1,)),
             dma((YS - 1,)), dma((YS - 1,)),
             dma((10,)), dma((10,)),
             dma((nz,)), dma((nz,)),
             dma((nz,)), dma((nz,)),
-            dma((3,)), dma((BUNDLES + 2,)),
+            dma((BUNDLES + 1,)), dma((BUNDLES + blocks,)),
         ],
         compiler_params=pltpu.CompilerParams(
             collective_id=0, has_side_effects=True, vmem_limit_bytes=60 * 1024 * 1024),
         name="layer",
-    )(patches, routed, qkv_weight)
-    grad_patches = gx.transpose(0, 2, 1).reshape(SEQ, feat)
-    grad_weight = fin[:blocks * width].reshape(blocks, width, LANES).transpose(0, 2, 1)
-    return grad_patches, grad_weight.reshape(d_model, width)
+    )(patches.T, grad_context.T, qkv_weight.T, counts[0])
+    return gx.T, fin.T
 
 
 def solution(mesh):

time: 132 us -> 121 us (0.917)
  local copies, waits for them, and re-layouts: 12.1 us -> 4.62 us
  other arithmetic: 1.85 us -> 0 us
    reshape x3 -> x0, local copies, waits for them, and re-layouts: 5.07 us -> none  [the longest x1 2.06 us: shards(): grad_patches = gx.transpose(0, 2, 1).reshape(SEQ, feat)]
    slice x1 -> x0, local copies, waits for them, and re-layouts: 1.47 us -> none  [shards(): fin[:blocks * width].reshape(blocks, width, LANES).transpose(0, 2, 1)]
    unnamed x7 -> x2, local copies, waits for them, and re-layouts: 5.58 us -> 4.62 us
where the time goes in v2:
time: 121 us
  Pallas kernels  116 us (96%)
  local copies, waits for them, and re-layouts  4.62 us (4%)
    pallas_call x1, Pallas kernels, shards(): pl.pallas_call(functools.partial(kernel, n_dp), out_shape=(jax.ShapeDtype...  116 us
    unnamed x2, local copies, waits for them, and re-layouts  4.62 us

profile of v2, /device:TPU:1, one launch (start us, length us, event | category | flops | bytes accessed | tf_op | source)
XLA Modules:
  0.0 121.3 jit_solution(10498935676543131463)
XLA Ops:
  0.6 116.0 %layer.1 = (bf16[352,1024]{1,0:T(8,128)(2,1)}, bf16[528,1408]{1,0:T(8,128)(2,1)}) custom-call(bf16[352,1024]{1,0:T(8,128)(2,1)} %bitcast.9, bf16[176,1024]{1,0:T(8,128)(2,1)} %bitcast.10, bf16[528,1408]{1,0:T(8,128)(2,1)} %bitcast.6, s32[4,4]{1,0:T(4,128)} %bitcast.11), custom_call_target="tpu_custom_call" | custom-call | tf_op jit(solution)/shard_map/layer/pallas_call | solution.py:411
  116.6 2.0 %copy.8 = bf16[1024,352]{0,1:T(8,128)(2,1)} copy(bf16[1024,352]{0,1:T(8,128)(2,1)} %bitcast.8) | data formatting | bytes 1441792
  118.7 2.6 %copy.9 = bf16[1408,528]{0,1:T(8,128)(2,1)} copy(bf16[1408,528]{0,1:T(8,128)(2,1)} %bitcast.7) | data formatting | bytes 2973696

commit v3 on v2

--- a/solution.py
+++ b/solution.py
@@ -17,6 +17,7 @@
 XS = 4
 CORES = 2
 LANES = 128
+SETS = 3
 TAG = 16
 
 F32 = jnp.float32
@@ -42,7 +43,8 @@
     stride = n_dp // BUNDLES
     scale = 1.0 / math.sqrt(HD)
     norm = 1.0 / math.sqrt(n_dp)
-    half = fin.shape[0] // 2
+    part = fin.shape[0] // SETS
+    half = part // CORES
     sub = half // 2
     q1 = sub // 2
     q2 = q1 // 2
@@ -137,35 +139,61 @@
         r = rows(core * fh, fh)
         return remote(wfb.at[who, r], wfb.at[who, r], v_ss.at[k - 1], v_rs.at[k - 1], mate)
 
-    own = core * half
-    oa, ob = own, own + sub
-    keep_a, keep_b = oa + bit1 * q1, ob + bit2 * q1
-    fa, fb = keep_a + bit2 * q2, keep_b + bit1 * q2
-    core_rs = remote(dw.at[rows((1 - core) * half, half)], c0, d_ss.at[0], d_rs.at[0], mate)
-    a1 = remote(dw.at[rows(oa + (1 - bit1) * q1, q1)], ra1, d_ss.at[1], d_rs.at[1], near1)
-    b1 = remote(dw.at[rows(ob + (1 - bit2) * q1, q1)], rb1, d_ss.at[2], d_rs.at[2], near2)
-    give_a2, give_b2 = keep_a + (1 - bit2) * q2, keep_b + (1 - bit1) * q2
-    a2 = remote(dw.at[rows(give_a2, q2)], ra2, d_ss.at[3], d_rs.at[3], near2)
-    b2 = remote(dw.at[rows(give_b2, q2)], rb2, d_ss.at[4], d_rs.at[4], near1)
-
-    def z_copy(k):
+    def spans(s):
+        oa = s * part + core * half
+        ob = oa + sub
+        keep_a, keep_b = oa + bit1 * q1, ob + bit2 * q1
+        return oa, ob, keep_a, keep_b, keep_a + bit2 * q2, keep_b + bit1 * q2
+
+    def core_sum(s):
+        r = rows(s * part + (1 - core) * half, half)
+        return remote(dw.at[r], c0.at[s], d_ss.at[s, 0], d_rs.at[s, 0], mate)
+
+    def x_sum1(s):
+        oa, ob = spans(s)[:2]
+        ra, rb = rows(oa + (1 - bit1) * q1, q1), rows(ob + (1 - bit2) * q1, q1)
+        return (
+            remote(dw.at[ra], ra1.at[s], d_ss.at[s, 1], d_rs.at[s, 1], near1),
+            remote(dw.at[rb], rb1.at[s], d_ss.at[s, 2], d_rs.at[s, 2], near2),
+        )
+
+    def gives(s):
+        keep_a, keep_b = spans(s)[2:4]
+        return keep_a + (1 - bit2) * q2, keep_b + (1 - bit1) * q2
+
+    def x_sum2(s):
+        ga, gb_ = gives(s)
+        return (
+            remote(dw.at[rows(ga, q2)], ra2.at[s], d_ss.at[s, 3], d_rs.at[s, 3], near2),
+            remote(dw.at[rows(gb_, q2)], rb2.at[s], d_ss.at[s, 4], d_rs.at[s, 4], near1),
+        )
+
+    def z_copy(s, k):
         to = (zi + k) % nz
-        return remote(ze.at[rows(to * piece, piece)], zr.at[k], z_ss.at[k], z_rs.at[k], z_peer(k))
-
-    def spot(z):
-        return jnp.where(z < nz // 2, fa + z * piece, fb + (z - nz // 2) * piece)
-
-    def f_copy(k):
-        r = rows(spot(zi), piece)
-        return remote(fin.at[r], fin.at[r], f_ss.at[k], f_rs.at[k], z_peer(k))
-
-    def same(start, size, i, dev):
+        return remote(ze.at[s, rows(to * piece, piece)], zr.at[s, k], z_ss.at[s, k], z_rs.at[s, k], z_peer(k))
+
+    def spot(s):
+        fa, fb = spans(s)[4:]
+        return jnp.where(zi < nz // 2, fa + zi * piece, fb + (zi - nz // 2) * piece)
+
+    def f_copy(s, k):
+        r = rows(spot(s), piece)
+        return remote(fin.at[r], fin.at[r], f_ss.at[s, k], f_rs.at[s, k], z_peer(k))
+
+    def same(s, start, size, i, dev):
         r = rows(start, size)
-        return remote(fin.at[r], fin.at[r], d_ss.at[i], d_rs.at[i], dev)
-
-    ag_a2, ag_b2 = same(fa, q2, 5, near2), same(fb, q2, 6, near1)
-    ag_a1, ag_b1 = same(keep_a, q1, 7, near1), same(keep_b, q1, 8, near2)
-    ag_core = same(own, half, 9, mate)
+        return remote(fin.at[r], fin.at[r], d_ss.at[s, i], d_rs.at[s, i], dev)
+
+    def x_gather2(s):
+        fa, fb = spans(s)[4:]
+        return same(s, fa, q2, 5, near2), same(s, fb, q2, 6, near1)
+
+    def x_gather1(s):
+        keep_a, keep_b = spans(s)[2:4]
+        return same(s, keep_a, q1, 7, near1), same(s, keep_b, q1, 8, near2)
+
+    def core_gather(s):
+        return (same(s, s * part + core * half, half, 9, mate),)
 
     barrier = pltpu.get_barrier_semaphore()
     mesh_id = pl.DeviceIdType.MESH
@@ -282,102 +310,130 @@
         dw[rows(at + width, width), :] = total[:, LANES:]
         return 0
 
-    lax.fori_loop(0, xt.shape[1] // (2 * LANES), weight_block, 0)
-    core_rs.start()
-
+    n_blocks = xt.shape[1] // (2 * LANES)
+    for s in range(SETS):
+        lax.fori_loop(s * n_blocks // SETS, (s + 1) * n_blocks // SETS, weight_block, 0)
+        core_sum(s).start()
+
+    def add_into(at, got, got_at, size):
+        dw[rows(at, size), :] += got[rows(got_at, size), :]
+
+    def add_core(s):
+        core_sum(s).wait_recv()
+        add_into(s * part + core * half, c0.at[s], 0, half)
+
+    def add_x1(s):
+        arrive(x_sum1(s))
+        ga, gb_ = gives(s)
+        fa, fb = spans(s)[4:]
+        add_into(ga, ra1.at[s], (1 - bit2) * q2, q2)
+        add_into(gb_, rb1.at[s], (1 - bit1) * q2, q2)
+        start(x_sum2(s))
+        add_into(fa, ra1.at[s], bit2 * q2, q2)
+        add_into(fb, rb1.at[s], bit1 * q2, q2)
+
+    def loop_z(f):
+        def body(k, _):
+            f(k)
+            return 0
+
+        lax.fori_loop(1, nz, body, 0)
+
+    def add_x2(s):
+        arrive(x_sum2(s))
+        fa, fb = spans(s)[4:]
+        ze[s, 0:q2, :] = dw[rows(fa, q2), :] + ra2[s]
+        ze[s, q2:2 * q2, :] = dw[rows(fb, q2), :] + rb2[s]
+        loop_z(lambda k: z_copy(s, k).start())
+
+    def add_z(s):
+        loop_z(lambda k: z_copy(s, k).wait_recv())
+        total = ze[s, rows(zi * piece, piece), :]
+        for k in range(1, nz):
+            total += zr[s, k]
+        fin[rows(spot(s), piece), :] = (total * norm).astype(BF16)
+        loop_z(lambda k: f_copy(s, k).start())
+
+    def pass_on(i):
+        arrive(p_copies(order(i)))
+        start(p_relays(order(i)))
+
+    def gx_copy(b):
+        return pltpu.make_async_copy(gxv.at[b], gx_hbm.at[:, cols(b)], o_sem.at[b])
+
+    def rows_grad(i):
+        b = order(i)
+        arrive(p_relays(b))
+        gxv[b] = dot(wf[...], gp[b], ((1,), (0,))).astype(BF16)
+        gx_copy(b).start()
+
+    def gathered_z(s):
+        loop_z(lambda k: f_copy(s, k).wait_recv())
+        start(x_gather2(s))
+
+    def gathered_x2(s):
+        arrive(x_gather2(s))
+        start(x_gather1(s))
+
+    def gathered_x1(s):
+        arrive(x_gather1(s))
+        start(core_gather(s))
+
+    def fin_out(n):
+        return pltpu.make_async_copy(
+            fin.at[n * width:(n + 1) * width], fin_hbm.at[:, n * LANES:(n + 1) * LANES],
+            o_sem.at[BUNDLES + n])
+
+    def whole_blocks(s):
+        return min(d_model // LANES, s * part // width)
+
+    def gathered_core(s):
+        arrive(core_gather(s))
+        for n in range(whole_blocks(s), whole_blocks(s + 1)):
+            fin_out(n).start()
+
+    add_core(0)
+    start(x_sum1(0))
+    add_core(1)
+    start(x_sum1(1))
+    add_core(2)
+    add_x1(0)
+    start(x_sum1(2))
+    add_x1(1)
+    add_x2(0)
+    add_x1(2)
+    add_x2(1)
     for k in range(1, YS):
         w_copy(k).wait_recv()
         v_copy(k).start()
-    core_rs.wait_recv()
-
-    def add_core(n, _):
-        r = rows(own + n * q2, q2)
-        dw[r, :] += c0[rows(n * q2, q2), :]
-        return 0
-
-    lax.fori_loop(0, half // q2, add_core, 0)
-    a1.start()
-    b1.start()
-
+    add_x2(2)
+    pass_on(0)
+    pass_on(1)
     for k in range(1, YS):
         v_copy(k).wait_recv()
     for j in range(YS):
         wf[:, j * width:(j + 1) * width] = wfb[j]
-
-    a1.wait_recv()
-    b1.wait_recv()
-
-    def add_into(at, got, got_at, size):
-        dw[rows(at, size), :] += got[rows(got_at, size), :]
-
-    add_into(give_a2, ra1, (1 - bit2) * q2, q2)
-    add_into(give_b2, rb1, (1 - bit1) * q2, q2)
-    a2.start()
-    b2.start()
-    add_into(fa, ra1, bit2 * q2, q2)
-    add_into(fb, rb1, bit1 * q2, q2)
-
-    for i in range(2):
-        arrive(p_copies(order(i)))
-        start(p_relays(order(i)))
-
-    a2.wait_recv()
-    b2.wait_recv()
-    ze[0:q2, :] = dw[rows(fa, q2), :] + ra2[...]
-    ze[q2:2 * q2, :] = dw[rows(fb, q2), :] + rb2[...]
-
-    def loop_z(f):
-        def body(k, _):
-            f(k)
-            return 0
-
-        lax.fori_loop(1, nz, body, 0)
-
-    loop_z(lambda k: z_copy(k).start())
-
-    for i in range(2, BUNDLES):
-        arrive(p_copies(order(i)))
-        start(p_relays(order(i)))
-
-    def gx_copy(b):
-        return pltpu.make_async_copy(gxv.at[b], gx_hbm.at[:, cols(b)], o_sem.at[b])
-
-    def rows_grad(i, _):
-        b = order(i)
-        arrive(p_relays(b))
-        gxv[b] = dot(wf[...], gp[b], ((1,), (0,))).astype(BF16)
-        gx_copy(b).start()
-        return 0
-
-    lax.fori_loop(0, BUNDLES, rows_grad, 0)
-
-    loop_z(lambda k: z_copy(k).wait_recv())
-
-    def add_z(k, total):
-        return total + zr[k]
-
-    total = lax.fori_loop(1, nz, add_z, ze[rows(zi * piece, piece), :])
-    fin[rows(spot(zi), piece), :] = (total * norm).astype(BF16)
-    loop_z(lambda k: f_copy(k).start())
-    loop_z(lambda k: f_copy(k).wait_recv())
-    ag_a2.start()
-    ag_b2.start()
-    ag_a2.wait_recv()
-    ag_b2.wait_recv()
-    ag_a1.start()
-    ag_b1.start()
-    ag_a1.wait_recv()
-    ag_b1.wait_recv()
-    ag_core.start()
-
-    def fin_out(n):
-        return pltpu.make_async_copy(
-            fin.at[n * width:(n + 1) * width], fin_hbm.at[:, n * LANES:(n + 1) * LANES],
-            o_sem.at[BUNDLES + n])
-
-    ag_core.wait_recv()
-    for n in range(d_model // LANES):
-        fin_out(n).start()
+    add_z(0)
+    pass_on(2)
+    add_z(1)
+    pass_on(3)
+    add_z(2)
+    gathered_z(0)
+    rows_grad(0)
+    gathered_z(1)
+    gathered_x2(0)
+    rows_grad(1)
+    gathered_x1(0)
+    gathered_x2(1)
+    rows_grad(2)
+    gathered_z(2)
+    gathered_x1(1)
+    gathered_core(0)
+    rows_grad(3)
+    gathered_x2(2)
+    gathered_core(1)
+    gathered_x1(2)
+    gathered_core(2)
 
     for b in range(BUNDLES):
         for cp in g_copy(b) + x_copies(b) + x_relays(b) + p_copies(b) + p_relays(b):
@@ -386,10 +442,12 @@
     for k in range(1, YS):
         w_copy(k).wait_send()
         v_copy(k).wait_send()
-    for cp in (core_rs, a1, b1, a2, b2, ag_a2, ag_b2, ag_a1, ag_b1, ag_core):
-        cp.wait_send()
-    loop_z(lambda k: z_copy(k).wait_send())
-    loop_z(lambda k: f_copy(k).wait_send())
+    for s in range(SETS):
+        for cp in x_sum1(s) + x_sum2(s) + x_gather2(s) + x_gather1(s) + core_gather(s):
+            cp.wait_send()
+        core_sum(s).wait_send()
+        loop_z(lambda k: z_copy(s, k).wait_send())
+        loop_z(lambda k: f_copy(s, k).wait_send())
     for n in range(d_model // LANES):
         fin_out(n).wait()
 
@@ -401,10 +459,10 @@
     d_model = YS * feat
     blocks = d_model // LANES
     parts = n_dp
-    unit = -(-(blocks * width) // (parts * 16)) * 16
+    unit = -(-(blocks * width) // (parts * SETS * 16)) * SETS * 16
     flat = unit * parts
     wide = 2 * LANES * (-(-blocks // 2))
-    half = flat // 2
+    half = flat // SETS // CORES
     q1, q2 = half // 4, half // 8
     dma = pltpu.SemaphoreType.DMA
     any_spec = pl.BlockSpec(memory_space=pl.ANY)
@@ -430,13 +488,13 @@
             pltpu.VMEM((YS, feat, width), BF16),
             pltpu.VMEM((feat, YS * width), BF16),
             pltpu.VMEM((max(flat, wide // LANES * width), LANES), F32),
-            pltpu.VMEM((half, LANES), F32),
-            pltpu.VMEM((q1, LANES), F32),
-            pltpu.VMEM((q2, LANES), F32),
-            pltpu.VMEM((q1, LANES), F32),
-            pltpu.VMEM((q2, LANES), F32),
-            pltpu.VMEM((2 * q2, LANES), F32),
-            pltpu.VMEM((nz, 2 * q2 // nz, LANES), F32),
+            pltpu.VMEM((SETS, half, LANES), F32),
+            pltpu.VMEM((SETS, q1, LANES), F32),
+            pltpu.VMEM((SETS, q2, LANES), F32),
+            pltpu.VMEM((SETS, q1, LANES), F32),
+            pltpu.VMEM((SETS, q2, LANES), F32),
+            pltpu.VMEM((SETS, 2 * q2, LANES), F32),
+            pltpu.VMEM((SETS, nz, 2 * q2 // nz, LANES), F32),
             pltpu.VMEM((flat, LANES), BF16),
             pltpu.VMEM((BUNDLES, feat, CAP), BF16),
             dma((4, BUNDLES)), dma((4, BUNDLES)),
@@ -445,9 +503,9 @@
             dma((4, BUNDLES)), dma((4, BUNDLES)),
             dma((YS - 1,)), dma((YS - 1,)),
             dma((YS - 1,)), dma((YS - 1,)),
-            dma((10,)), dma((10,)),
-            dma((nz,)), dma((nz,)),
-            dma((nz,)), dma((nz,)),
+            dma((SETS, 10)), dma((SETS, 10)),
+            dma((SETS, nz)), dma((SETS, nz)),
+            dma((SETS, nz)), dma((SETS, nz)),
             dma((BUNDLES + 1,)), dma((BUNDLES + blocks,)),
         ],
         compiler_params=pltpu.CompilerParams(

time: 121 us -> 115 us (0.950)
  the two profiles are of different devices: /device:TPU:1 before, /device:TPU:9 now
where the time goes in v3:
time: 115 us
  Pallas kernels  110 us (96%)
  local copies, waits for them, and re-layouts  4.62 us (4%)
    pallas_call x1, Pallas kernels, shards(): pl.pallas_call(functools.partial(kernel, n_dp), out_shape=(jax.ShapeDtype...  110 us
    unnamed x2, local copies, waits for them, and re-layouts  4.62 us

profile of v3, /device:TPU:9, one launch (start us, length us, event | category | flops | bytes accessed | tf_op | source)
XLA Modules:
  0.0 115.0 jit_solution(8863567775029977818)
XLA Ops:
  0.6 109.8 %layer.1 = (bf16[352,1024]{1,0:T(8,128)(2,1)}, bf16[528,1408]{1,0:T(8,128)(2,1)}) custom-call(bf16[352,1024]{1,0:T(8,128)(2,1)} %bitcast.9, bf16[176,1024]{1,0:T(8,128)(2,1)} %bitcast.10, bf16[528,1408]{1,0:T(8,128)(2,1)} %bitcast.6, s32[4,4]{1,0:T(4,128)} %bitcast.11), custom_call_target="tpu_custom_call" | custom-call | tf_op jit(solution)/shard_map/layer/pallas_call | solution.py:469
  110.4 2.0 %copy.8 = bf16[1024,352]{0,1:T(8,128)(2,1)} copy(bf16[1024,352]{0,1:T(8,128)(2,1)} %bitcast.8) | data formatting | bytes 1441792
  112.4 2.6 %copy.9 = bf16[1408,528]{0,1:T(8,128)(2,1)} copy(bf16[1408,528]{0,1:T(8,128)(2,1)} %bitcast.7) | data formatting | bytes 2973696

commit v4 on v3

--- a/solution.py
+++ b/solution.py
@@ -31,9 +31,9 @@
 def kernel(
     n_dp,
     x_hbm, g_hbm, w_hbm, counts,
-    gx_hbm, fin_hbm,
-    xt, wt, wn, tag, gt, gb, pk, up_all, gps, gp, wfb, wf, dw, c0, ra1, ra2, rb1, rb2, ze, zr, fin, gxv,
-    x_ss, x_rs, g_ss, g_rs, t_ss, t_rs, p_ss, p_rs, w_ss, w_rs, v_ss, v_rs, d_ss, d_rs, z_ss, z_rs, f_ss, f_rs, l_sem, o_sem,
+    gx_out, fin_out,
+    xt, wt, wn, tag, gt, gb, pk, up_all, gps, gp, wfb, wf, dw, c0, ra1, ra2, rb1, rb2, ze, rz, zh, zr, fin,
+    x_ss, x_rs, g_ss, g_rs, t_ss, t_rs, p_ss, p_rs, w_ss, w_rs, v_ss, v_rs, d_ss, d_rs, z_ss, z_rs, f_ss, f_rs, l_sem,
 ):
     feat = x_hbm.shape[0]
     width = w_hbm.shape[0]
@@ -48,6 +48,7 @@
     sub = half // 2
     q1 = sub // 2
     q2 = q1 // 2
+    q3 = q2 // 2
     piece = 2 * q2 // nz
 
     dp = lax.axis_index("dp")
@@ -64,6 +65,10 @@
     bit1 = ((xi + 1) // 2) % 2
     bit2 = xi // 2
 
+    par, zg = zi % 2, zi // 2
+    zn1 = {"dp": dp + (1 - 2 * par) * (XS * CORES)}
+    zn2 = {"dp": (dp + n_dp + (2 * par - 1) * (XS * CORES)) % n_dp}
+
     def z_peer(k):
         return {"dp": ((zi + k) % nz) * (XS * CORES) + xi * CORES + core}
 
@@ -168,13 +173,21 @@
             remote(dw.at[rows(gb_, q2)], rb2.at[s], d_ss.at[s, 4], d_rs.at[s, 4], near1),
         )
 
+    def z_half(s):
+        give = (1 - par) * q3
+        return (
+            remote(ze.at[s, rows(give, q3)], rz.at[s, 0:q3], d_ss.at[s, 10], d_rs.at[s, 10], zn1),
+            remote(ze.at[s, rows(q2 + give, q3)], rz.at[s, q3:2 * q3], d_ss.at[s, 11], d_rs.at[s, 11], zn2),
+        )
+
     def z_copy(s, k):
-        to = (zi + k) % nz
-        return remote(ze.at[s, rows(to * piece, piece)], zr.at[s, k], z_ss.at[s, k], z_rs.at[s, k], z_peer(k))
+        to = ((zi + 2 * k) % nz) // 2
+        return remote(zh.at[s, rows(to * piece, piece)], zr.at[s, k], z_ss.at[s, k], z_rs.at[s, k], z_peer(2 * k))
 
     def spot(s):
         fa, fb = spans(s)[4:]
-        return jnp.where(zi < nz // 2, fa + zi * piece, fb + (zi - nz // 2) * piece)
+        at = par * q3 + zg * piece
+        return jnp.where(zg < nz // 4, fa + at, fb + at - q3)
 
     def f_copy(s, k):
         r = rows(spot(s), piece)
@@ -344,12 +357,25 @@
         fa, fb = spans(s)[4:]
         ze[s, 0:q2, :] = dw[rows(fa, q2), :] + ra2[s]
         ze[s, q2:2 * q2, :] = dw[rows(fb, q2), :] + rb2[s]
-        loop_z(lambda k: z_copy(s, k).start())
+        start(z_half(s))
+
+    def loop_zz(f):
+        def body(k, _):
+            f(k)
+            return 0
+
+        lax.fori_loop(1, nz // 2, body, 0)
+
+    def add_z1(s):
+        arrive(z_half(s))
+        zh[s, 0:q3, :] = ze[s, rows(par * q3, q3), :] + rz[s, 0:q3, :]
+        zh[s, q3:2 * q3, :] = ze[s, rows(q2 + par * q3, q3), :] + rz[s, q3:2 * q3, :]
+        loop_zz(lambda k: z_copy(s, k).start())
 
     def add_z(s):
-        loop_z(lambda k: z_copy(s, k).wait_recv())
-        total = ze[s, rows(zi * piece, piece), :]
-        for k in range(1, nz):
+        loop_zz(lambda k: z_copy(s, k).wait_recv())
+        total = zh[s, rows(zg * piece, piece), :]
+        for k in range(1, nz // 2):
             total += zr[s, k]
         fin[rows(spot(s), piece), :] = (total * norm).astype(BF16)
         loop_z(lambda k: f_copy(s, k).start())
@@ -358,14 +384,10 @@
         arrive(p_copies(order(i)))
         start(p_relays(order(i)))
 
-    def gx_copy(b):
-        return pltpu.make_async_copy(gxv.at[b], gx_hbm.at[:, cols(b)], o_sem.at[b])
-
     def rows_grad(i):
         b = order(i)
         arrive(p_relays(b))
-        gxv[b] = dot(wf[...], gp[b], ((1,), (0,))).astype(BF16)
-        gx_copy(b).start()
+        gx_out[:, b * CAP:(b + 1) * CAP] = dot(wf[...], gp[b], ((1,), (0,))).astype(BF16)
 
     def gathered_z(s):
         loop_z(lambda k: f_copy(s, k).wait_recv())
@@ -379,18 +401,13 @@
         arrive(x_gather1(s))
         start(core_gather(s))
 
-    def fin_out(n):
-        return pltpu.make_async_copy(
-            fin.at[n * width:(n + 1) * width], fin_hbm.at[:, n * LANES:(n + 1) * LANES],
-            o_sem.at[BUNDLES + n])
-
     def whole_blocks(s):
         return min(d_model // LANES, s * part // width)
 
     def gathered_core(s):
         arrive(core_gather(s))
         for n in range(whole_blocks(s), whole_blocks(s + 1)):
-            fin_out(n).start()
+            fin_out[:, n * LANES:(n + 1) * LANES] = fin[n * width:(n + 1) * width, :]
 
     add_core(0)
     start(x_sum1(0))
@@ -402,11 +419,14 @@
     add_x1(1)
     add_x2(0)
     add_x1(2)
+    add_z1(0)
     add_x2(1)
     for k in range(1, YS):
         w_copy(k).wait_recv()
         v_copy(k).start()
     add_x2(2)
+    add_z1(1)
+    add_z1(2)
     pass_on(0)
     pass_on(1)
     for k in range(1, YS):
@@ -438,18 +458,15 @@
     for b in range(BUNDLES):
         for cp in g_copy(b) + x_copies(b) + x_relays(b) + p_copies(b) + p_relays(b):
             cp.wait_send()
-        gx_copy(b).wait()
     for k in range(1, YS):
         w_copy(k).wait_send()
         v_copy(k).wait_send()
     for s in range(SETS):
-        for cp in x_sum1(s) + x_sum2(s) + x_gather2(s) + x_gather1(s) + core_gather(s):
+        for cp in x_sum1(s) + x_sum2(s) + z_half(s) + x_gather2(s) + x_gather1(s) + core_gather(s):
             cp.wait_send()
         core_sum(s).wait_send()
-        loop_z(lambda k: z_copy(s, k).wait_send())
+        loop_zz(lambda k: z_copy(s, k).wait_send())
         loop_z(lambda k: f_copy(s, k).wait_send())
-    for n in range(d_model // LANES):
-        fin_out(n).wait()
 
 
 def shards(patches, counts, qkv_weight, grad_context):
@@ -464,16 +481,17 @@
     wide = 2 * LANES * (-(-blocks // 2))
     half = flat // SETS // CORES
     q1, q2 = half // 4, half // 8
+    operands = patches.T, grad_context.T, qkv_weight.T, counts[0]
     dma = pltpu.SemaphoreType.DMA
-    any_spec = pl.BlockSpec(memory_space=pl.ANY)
+    hbm_spec = pl.BlockSpec(memory_space=pltpu.HBM)
     gx, fin = pl.pallas_call(
         functools.partial(kernel, n_dp),
         out_shape=(
             jax.ShapeDtypeStruct((feat, SEQ), BF16),
             jax.ShapeDtypeStruct((width, d_model), BF16),
         ),
-        in_specs=[any_spec] * 3 + [pl.BlockSpec(memory_space=pltpu.SMEM)],
-        out_specs=(any_spec, any_spec),
+        in_specs=[hbm_spec] * 3 + [pl.BlockSpec(memory_space=pltpu.SMEM)],
+        out_specs=(pl.BlockSpec(memory_space=pltpu.VMEM),) * 2,
         scratch_shapes=[
             pltpu.VMEM((BUNDLES, wide, CAP), BF16),
             pltpu.VMEM((width, d_model), BF16),
@@ -494,24 +512,25 @@
             pltpu.VMEM((SETS, q1, LANES), F32),
             pltpu.VMEM((SETS, q2, LANES), F32),
             pltpu.VMEM((SETS, 2 * q2, LANES), F32),
-            pltpu.VMEM((SETS, nz, 2 * q2 // nz, LANES), F32),
+            pltpu.VMEM((SETS, q2, LANES), F32),
+            pltpu.VMEM((SETS, q2, LANES), F32),
+            pltpu.VMEM((SETS, nz // 2, 2 * q2 // nz, LANES), F32),
             pltpu.VMEM((flat, LANES), BF16),
-            pltpu.VMEM((BUNDLES, feat, CAP), BF16),
             dma((4, BUNDLES)), dma((4, BUNDLES)),
             dma((BUNDLES,)), dma((BUNDLES,)),
             dma((BUNDLES,)), dma((BUNDLES,)),
             dma((4, BUNDLES)), dma((4, BUNDLES)),
             dma((YS - 1,)), dma((YS - 1,)),
             dma((YS - 1,)), dma((YS - 1,)),
-            dma((SETS, 10)), dma((SETS, 10)),
+            dma((SETS, 12)), dma((SETS, 12)),
+            dma((SETS, nz // 2)), dma((SETS, nz // 2)),
             dma((SETS, nz)), dma((SETS, nz)),
-            dma((SETS, nz)), dma((SETS, nz)),
-            dma((BUNDLES + 1,)), dma((BUNDLES + blocks,)),
+            dma((BUNDLES + 1,)),
         ],
         compiler_params=pltpu.CompilerParams(
-            collective_id=0, has_side_effects=True, vmem_limit_bytes=60 * 1024 * 1024),
+            collective_id=0, has_side_effects=True, vmem_limit_bytes=50 * 1024 * 1024),
         name="layer",
-    )(patches.T, grad_context.T, qkv_weight.T, counts[0])
+    )(*[pltpu.with_memory_space_constraint(a, pltpu.HBM) for a in operands])
     return gx.T, fin.T
 
 

time: 115 us -> 110 us (0.957)
  Pallas kernels: 110 us -> 107 us
  local copies, waits for them, and re-layouts: 4.62 us -> 1.97 us
    unnamed x2, local copies, waits for them, and re-layouts: 4.62 us -> 1.97 us
    pallas_call x1, Pallas kernels: 110 us -> 107 us  [shards(): pl.pallas_call(functools.partial(kernel, n_dp), out_shape=(jax.ShapeDtype...]
where the time goes in v4:
time: 110 us
  Pallas kernels  107 us (97%)
  local copies, waits for them, and re-layouts  1.97 us (2%)
    pallas_call x1, Pallas kernels, shards(): pl.pallas_call(functools.partial(kernel, n_dp), out_shape=(jax.ShapeDtype...  107 us

profile of v4, /device:TPU:9, one launch (start us, length us, event | category | flops | bytes accessed | tf_op | source)
XLA Modules:
  0.0 110.0 jit_solution(5823187854857149712)
XLA Ops:
  0.6 107.4 %layer.1 = (bf16[352,1024]{1,0:T(8,128)(2,1)S(1)}, bf16[528,1408]{1,0:T(8,128)(2,1)S(1)}) custom-call(bf16[352,1024]{1,0:T(8,128)(2,1)} %bitcast.9, bf16[176,1024]{1,0:T(8,128)(2,1)} %bitcast.10, bf16[528,1408]{1,0:T(8,128)(2,1)} %bitcast.8, s32[4,4]{1,0:T(4,128)} %bitcast.11), custom_call_target="tpu_custom_call" | custom-call | tf_op jit(solution)/shard_map/layer/pallas_call | solution.py:487
  108.0 0.9 copy.8
  108.9 1.1 %copy.9 = bf16[1408,528]{0,1:T(8,128)(2,1)} copy(bf16[1408,528]{0,1:T(8,128)(2,1)S(1)} %bitcast.6) | data formatting | bytes 2973696

commit v5 on v4

--- a/solution.py
+++ b/solution.py
@@ -33,7 +33,7 @@
     x_hbm, g_hbm, w_hbm, counts,
     gx_out, fin_out,
     xt, wt, wn, tag, gt, gb, pk, up_all, gps, gp, wfb, wf, dw, c0, ra1, ra2, rb1, rb2, ze, rz, zh, zr, fin,
-    x_ss, x_rs, g_ss, g_rs, t_ss, t_rs, p_ss, p_rs, w_ss, w_rs, v_ss, v_rs, d_ss, d_rs, z_ss, z_rs, f_ss, f_rs, l_sem,
+    x_ss, x_rs, g_ss, g_rs, t_ss, t_rs, p_ss, p_rs, w_ss, w_rs, v_ss, v_rs, d_ss, d_rs, z_ss, z_rs, f_ss, f_rs, l_sem, word,
 ):
     feat = x_hbm.shape[0]
     width = w_hbm.shape[0]
@@ -211,12 +211,7 @@
     barrier = pltpu.get_barrier_semaphore()
     mesh_id = pl.DeviceIdType.MESH
 
-    def greet(k, _):
-        pl.semaphore_signal(barrier, inc=1, device_id=z_peer(k), device_id_type=mesh_id)
-        return 0
-
-    lax.fori_loop(1, nz, greet, 0)
-    for dev in [{"mp": right}, {"mp": left}, {"mp": far}, mate, near1, near2]:
+    for dev in [{"mp": right}, {"mp": left}, mate, near1, near2, zn1, zn2]:
         pl.semaphore_signal(barrier, inc=1, device_id=dev, device_id_type=mesh_id)
     w_local = pltpu.make_async_copy(w_hbm, wt, l_sem.at[BUNDLES])
     w_local.start()
@@ -233,7 +228,14 @@
         tag[b] = jnp.where(slot < end, ids - IMGS, slot).astype(F32).astype(BF16)
     for b in range(BUNDLES):
         xt[b, d_model:, :] = jnp.zeros((xt.shape[1] - d_model, CAP), BF16)
-    pl.semaphore_wait(barrier, 6 + nz - 1)
+    pl.semaphore_wait(barrier, 7)
+
+    def tell(i):
+        for k in (2 ** i, nz - 2 ** i):
+            pl.semaphore_signal(word.at[i], inc=1, device_id=z_peer(k), device_id_type=mesh_id)
+
+    def hear(i):
+        pl.semaphore_wait(word.at[i], 2)
 
     def start(copies):
         for cp in copies:
@@ -244,19 +246,42 @@
             cp.wait_recv()
 
     start(x_copies(0))
-    for i in range(BUNDLES):
-        start(g_copy(order(i)))
     start(x_copies(order(1)))
+    tell(0)
     w_local.wait()
     for n in range(d_model // LANES):
         wn[n * LANES:(n + 1) * LANES, :] = wt[:, n * LANES:(n + 1) * LANES].T
+    hear(0)
+    tell(1)
+    start(g_copy(order(0)))
+    start(g_copy(order(1)))
     for i in range(BUNDLES):
         x_local(order(i)).wait()
     wfb[me] = wn[rows(me * feat, feat), :]
+    hear(1)
+    tell(2)
 
     arrive(x_copies(0))
     start(x_relays(0))
     start(x_copies(order(2)))
+    hear(2)
+    start(g_copy(order(2)))
+    start(g_copy(order(3)))
+
+    mine = rows(me * width, width)
+    n_blocks = xt.shape[1] // (2 * LANES)
+
+    def weight_term(n, b):
+        return dot(gp[b, mine, :], xt[b, rows(n * 2 * LANES, 2 * LANES), :], ((1,), (1,)))
+
+    def first_blocks(n, _):
+        total = weight_term(n, order(0))
+        for i in range(1, BUNDLES - 1):
+            total += weight_term(n, order(i))
+        at = n * 2 * width
+        dw[rows(at, width), :] = total[:, :LANES]
+        dw[rows(at + width, width), :] = total[:, LANES:]
+        return 0
 
     def bundle(i, _):
         b = order(i)
@@ -281,6 +306,7 @@
         @pl.when(i == 3)
         def _():
             start(p_copies(order(2)))
+            lax.fori_loop(0, n_blocks, first_blocks, 0)
 
         arrive(x_relays(b))
         pk[...] = dot(wt[...], xt[b, 0:d_model, :], ((1,), (0,)))
@@ -311,19 +337,13 @@
     lax.fori_loop(0, BUNDLES, bundle, 0)
     start(p_copies(order(3)))
 
-    mine = rows(me * width, width)
-
     def weight_block(n, _):
-        block = rows(n * 2 * LANES, 2 * LANES)
-        total = dot(gp[0, mine, :], xt[0, block, :], ((1,), (1,)))
-        for b in range(1, BUNDLES):
-            total += dot(gp[b, mine, :], xt[b, block, :], ((1,), (1,)))
+        total = weight_term(n, order(BUNDLES - 1))
         at = n * 2 * width
-        dw[rows(at, width), :] = total[:, :LANES]
-        dw[rows(at + width, width), :] = total[:, LANES:]
+        dw[rows(at, width), :] += total[:, :LANES]
+        dw[rows(at + width, width), :] += total[:, LANES:]
         return 0
 
-    n_blocks = xt.shape[1] // (2 * LANES)
     for s in range(SETS):
         lax.fori_loop(s * n_blocks // SETS, (s + 1) * n_blocks // SETS, weight_block, 0)
         core_sum(s).start()
@@ -526,6 +546,7 @@
             dma((SETS, nz // 2)), dma((SETS, nz // 2)),
             dma((SETS, nz)), dma((SETS, nz)),
             dma((BUNDLES + 1,)),
+            pltpu.SemaphoreType.REGULAR((3,)),
         ],
         compiler_params=pltpu.CompilerParams(
             collective_id=0, has_side_effects=True, vmem_limit_bytes=50 * 1024 * 1024),

time: 110 us -> 107 us (0.973)
  the two profiles are of different devices: /device:TPU:9 before, /device:TPU:1 now
where the time goes in v5:
time: 107 us; the launch traced here: 106 us
  Pallas kernels  104 us (97%)
  local copies, waits for them, and re-layouts  1.97 us (2%)
    pallas_call x1, Pallas kernels, shards(): pl.pallas_call(functools.partial(kernel, n_dp), out_shape=(jax.ShapeDtype...  104 us

profile of v5, /device:TPU:1, one launch (start us, length us, event | category | flops | bytes accessed | tf_op | source)
XLA Modules:
  0.0 106.1 jit_solution(17963271906630209808)
XLA Ops:
  0.6 103.5 %layer.1 = (bf16[352,1024]{1,0:T(8,128)(2,1)S(1)}, bf16[528,1408]{1,0:T(8,128)(2,1)S(1)}) custom-call(bf16[352,1024]{1,0:T(8,128)(2,1)} %bitcast.9, bf16[176,1024]{1,0:T(8,128)(2,1)} %bitcast.10, bf16[528,1408]{1,0:T(8,128)(2,1)} %bitcast.8, s32[4,4]{1,0:T(4,128)} %bitcast.11), custom_call_target="tpu_custom_call" | custom-call | tf_op jit(solution)/shard_map/layer/pallas_call | solution.py:507
  104.1 0.9 copy.8
  105.0 1.1 %copy.9 = bf16[1408,528]{0,1:T(8,128)(2,1)} copy(bf16[1408,528]{0,1:T(8,128)(2,1)S(1)} %bitcast.6) | data formatting | bytes 2973696

commit v6 on v5

--- a/solution.py
+++ b/solution.py
@@ -463,16 +463,16 @@
     gathered_z(1)
     gathered_x2(0)
     rows_grad(1)
-    gathered_x1(0)
+    gathered_z(2)
     gathered_x2(1)
     rows_grad(2)
-    gathered_z(2)
+    gathered_x1(0)
+    gathered_x2(2)
+    rows_grad(3)
     gathered_x1(1)
     gathered_core(0)
-    rows_grad(3)
-    gathered_x2(2)
+    gathered_x1(2)
     gathered_core(1)
-    gathered_x1(2)
     gathered_core(2)
 
     for b in range(BUNDLES):

time: 107 us -> 102 us (0.953)
  Pallas kernels: 104 us -> 99.5 us
    pallas_call x1, Pallas kernels: 104 us -> 99.5 us  [shards(): pl.pallas_call(functools.partial(kernel, n_dp), out_shape=(jax.ShapeDtype...]
where the time goes in v6:
time: 102 us
  Pallas kernels  99.5 us (98%)
  local copies, waits for them, and re-layouts  1.97 us (2%)
    pallas_call x1, Pallas kernels, shards(): pl.pallas_call(functools.partial(kernel, n_dp), out_shape=(jax.ShapeDtype...  99.5 us

profile of v6, /device:TPU:1, one launch (start us, length us, event | category | flops | bytes accessed | tf_op | source)
XLA Modules:
  0.0 102.1 jit_solution(6623250193617891728)
XLA Ops:
  0.6 99.5 %layer.1 = (bf16[352,1024]{1,0:T(8,128)(2,1)S(1)}, bf16[528,1408]{1,0:T(8,128)(2,1)S(1)}) custom-call(bf16[352,1024]{1,0:T(8,128)(2,1)} %bitcast.9, bf16[176,1024]{1,0:T(8,128)(2,1)} %bitcast.10, bf16[528,1408]{1,0:T(8,128)(2,1)} %bitcast.8, s32[4,4]{1,0:T(4,128)} %bitcast.11), custom_call_target="tpu_custom_call" | custom-call | tf_op jit(solution)/shard_map/layer/pallas_call | solution.py:507
  100.1 0.9 copy.8
  101.0 1.1 %copy.9 = bf16[1408,528]{0,1:T(8,128)(2,1)} copy(bf16[1408,528]{0,1:T(8,128)(2,1)S(1)} %bitcast.6) | data formatting | bytes 2973696

commit v7 on v6

--- a/solution.py
+++ b/solution.py
@@ -32,7 +32,7 @@
     n_dp,
     x_hbm, g_hbm, w_hbm, counts,
     gx_out, fin_out,
-    xt, wt, wn, tag, gt, gb, pk, up_all, gps, gp, wfb, wf, dw, c0, ra1, ra2, rb1, rb2, ze, rz, zh, zr, fin,
+    xt, wt, wn, tag, gt, gb, pk, up_all, gps, gp, wfb, wf, dw, c0, ra1, ra2, rb1, rb2, ze, rz, zh, zf, zr, fin,
     x_ss, x_rs, g_ss, g_rs, t_ss, t_rs, p_ss, p_rs, w_ss, w_rs, v_ss, v_rs, d_ss, d_rs, z_ss, z_rs, f_ss, f_rs, l_sem, word,
 ):
     feat = x_hbm.shape[0]
@@ -183,6 +183,13 @@
     def z_copy(s, k):
         to = ((zi + 2 * k) % nz) // 2
         return remote(zh.at[s, rows(to * piece, piece)], zr.at[s, k], z_ss.at[s, k], z_rs.at[s, k], z_peer(2 * k))
+
+    def far_copy(s):
+        to = ((zi + nz // 2) % nz) // 2
+        return remote(zh.at[s, rows(to * piece, piece)], zf.at[s], d_ss.at[s, 12], d_rs.at[s, 12], z_peer(nz - nz // 4))
+
+    direct = [k for k in range(1, nz // 2) if k not in (nz // 4, nz // 2 - nz // 8)]
+    last = nz // 2 - nz // 8
 
     def spot(s):
         fa, fb = spans(s)[4:]
@@ -379,23 +386,25 @@
         ze[s, q2:2 * q2, :] = dw[rows(fb, q2), :] + rb2[s]
         start(z_half(s))
 
-    def loop_zz(f):
-        def body(k, _):
-            f(k)
-            return 0
-
-        lax.fori_loop(1, nz // 2, body, 0)
-
     def add_z1(s):
         arrive(z_half(s))
         zh[s, 0:q3, :] = ze[s, rows(par * q3, q3), :] + rz[s, 0:q3, :]
         zh[s, q3:2 * q3, :] = ze[s, rows(q2 + par * q3, q3), :] + rz[s, q3:2 * q3, :]
-        loop_zz(lambda k: z_copy(s, k).start())
+        far_copy(s).start()
+        for k in direct:
+            z_copy(s, k).start()
+
+    def pass_far(s):
+        far_copy(s).wait_recv()
+        r = rows(((zi + 2 * last) % nz) // 2 * piece, piece)
+        zh[s, r, :] += zf[s]
+        z_copy(s, last).start()
 
     def add_z(s):
-        loop_zz(lambda k: z_copy(s, k).wait_recv())
         total = zh[s, rows(zg * piece, piece), :]
-        for k in range(1, nz // 2):
+        for k in direct + [last]:
+            z_copy(s, k).wait_recv()
+        for k in direct + [last]:
             total += zr[s, k]
         fin[rows(spot(s), piece), :] = (total * norm).astype(BF16)
         loop_z(lambda k: f_copy(s, k).start())
@@ -428,6 +437,27 @@
         arrive(core_gather(s))
         for n in range(whole_blocks(s), whole_blocks(s + 1)):
             fin_out[:, n * LANES:(n + 1) * LANES] = fin[n * width:(n + 1) * width, :]
+
+    def early_sends_left():
+        for b in range(BUNDLES):
+            for cp in g_copy(b) + x_copies(b) + x_relays(b) + p_copies(b) + p_relays(b):
+                cp.wait_send()
+        for k in range(1, YS):
+            w_copy(k).wait_send()
+            v_copy(k).wait_send()
+        for s in range(SETS):
+            for cp in x_sum1(s) + x_sum2(s) + z_half(s) + x_gather2(s):
+                cp.wait_send()
+            core_sum(s).wait_send()
+            far_copy(s).wait_send()
+            for k in direct + [last]:
+                z_copy(s, k).wait_send()
+            loop_z(lambda k: f_copy(s, k).wait_send())
+
+    def late_sends_left(sets):
+        for s in sets:
+            for cp in x_gather1(s) + core_gather(s):
+                cp.wait_send()
 
     add_core(0)
     start(x_sum1(0))
@@ -445,6 +475,7 @@
         w_copy(k).wait_recv()
         v_copy(k).start()
     add_x2(2)
+    pass_far(0)
     add_z1(1)
     add_z1(2)
     pass_on(0)
@@ -453,7 +484,9 @@
         v_copy(k).wait_recv()
     for j in range(YS):
         wf[:, j * width:(j + 1) * width] = wfb[j]
+    pass_far(1)
     add_z(0)
+    pass_far(2)
     pass_on(2)
     add_z(1)
     pass_on(3)
@@ -471,22 +504,12 @@
     rows_grad(3)
     gathered_x1(1)
     gathered_core(0)
+    early_sends_left()
     gathered_x1(2)
     gathered_core(1)
+    late_sends_left(range(SETS - 1))
     gathered_core(2)
-
-    for b in range(BUNDLES):
-        for cp in g_copy(b) + x_copies(b) + x_relays(b) + p_copies(b) + p_relays(b):
-            cp.wait_send()
-    for k in range(1, YS):
-        w_copy(k).wait_send()
-        v_copy(k).wait_send()
-    for s in range(SETS):
-        for cp in x_sum1(s) + x_sum2(s) + z_half(s) + x_gather2(s) + x_gather1(s) + core_gather(s):
-            cp.wait_send()
-        core_sum(s).wait_send()
-        loop_zz(lambda k: z_copy(s, k).wait_send())
-        loop_z(lambda k: f_copy(s, k).wait_send())
+    late_sends_left([SETS - 1])
 
 
 def shards(patches, counts, qkv_weight, grad_context):
@@ -534,6 +557,7 @@
             pltpu.VMEM((SETS, 2 * q2, LANES), F32),
             pltpu.VMEM((SETS, q2, LANES), F32),
             pltpu.VMEM((SETS, q2, LANES), F32),
+            pltpu.VMEM((SETS, 2 * q2 // nz, LANES), F32),
             pltpu.VMEM((SETS, nz // 2, 2 * q2 // nz, LANES), F32),
             pltpu.VMEM((flat, LANES), BF16),
             dma((4, BUNDLES)), dma((4, BUNDLES)),
@@ -542,7 +566,7 @@
             dma((4, BUNDLES)), dma((4, BUNDLES)),
             dma((YS - 1,)), dma((YS - 1,)),
             dma((YS - 1,)), dma((YS - 1,)),
-            dma((SETS, 12)), dma((SETS, 12)),
+            dma((SETS, 13)), dma((SETS, 13)),
             dma((SETS, nz // 2)), dma((SETS, nz // 2)),
             dma((SETS, nz)), dma((SETS, nz)),
             dma((BUNDLES + 1,)),

time: 102 us -> 103 us (level)
  no operation moved by 1% of the time
where the time goes in v7:
time: 103 us; the launch traced here: 102 us
  Pallas kernels  99.5 us (97%)
  local copies, waits for them, and re-layouts  1.97 us (2%)
    pallas_call x1, Pallas kernels, shards(): pl.pallas_call(functools.partial(kernel, n_dp), out_shape=(jax.ShapeDtype...  99.5 us

profile of v7, /device:TPU:1, one launch (start us, length us, event | category | flops | bytes accessed | tf_op | source)
XLA Modules:
  0.0 102.1 jit_solution(12596465015802855825)
XLA Ops:
  0.6 99.5 %layer.1 = (bf16[352,1024]{1,0:T(8,128)(2,1)S(1)}, bf16[528,1408]{1,0:T(8,128)(2,1)S(1)}) custom-call(bf16[352,1024]{1,0:T(8,128)(2,1)} %bitcast.9, bf16[176,1024]{1,0:T(8,128)(2,1)} %bitcast.10, bf16[528,1408]{1,0:T(8,128)(2,1)} %bitcast.8, s32[4,4]{1,0:T(4,128)} %bitcast.11), custom_call_target="tpu_custom_call" | custom-call | tf_op jit(solution)/shard_map/layer/pallas_call | solution.py:530
  100.1 0.9 copy.8
  101.0 1.1 %copy.9 = bf16[1408,528]{0,1:T(8,128)(2,1)} copy(bf16[1408,528]{0,1:T(8,128)(2,1)S(1)} %bitcast.6) | data formatting | bytes 2973696

commit v8 on v7

--- a/solution.py
+++ b/solution.py
@@ -487,20 +487,20 @@
     pass_far(1)
     add_z(0)
     pass_far(2)
+    add_z(1)
     pass_on(2)
-    add_z(1)
+    add_z(2)
     pass_on(3)
-    add_z(2)
     gathered_z(0)
-    rows_grad(0)
     gathered_z(1)
     gathered_x2(0)
-    rows_grad(1)
+    rows_grad(0)
     gathered_z(2)
     gathered_x2(1)
+    rows_grad(1)
     rows_grad(2)
+    gathered_x2(2)
     gathered_x1(0)
-    gathered_x2(2)
     rows_grad(3)
     gathered_x1(1)
     gathered_core(0)

time: 103 us -> 103 us (level)
  no operation moved by 1% of the time
where the time goes in v8:
time: 103 us
  Pallas kernels  100 us (97%)
  local copies, waits for them, and re-layouts  1.97 us (2%)
    pallas_call x1, Pallas kernels, shards(): pl.pallas_call(functools.partial(kernel, n_dp), out_shape=(jax.ShapeDtype...  100 us

profile of v8, /device:TPU:1, one launch (start us, length us, event | category | flops | bytes accessed | tf_op | source)
XLA Modules:
  0.0 102.7 jit_solution(6496112768785376154)
XLA Ops:
  0.6 100.1 %layer.1 = (bf16[352,1024]{1,0:T(8,128)(2,1)S(1)}, bf16[528,1408]{1,0:T(8,128)(2,1)S(1)}) custom-call(bf16[352,1024]{1,0:T(8,128)(2,1)} %bitcast.9, bf16[176,1024]{1,0:T(8,128)(2,1)} %bitcast.10, bf16[528,1408]{1,0:T(8,128)(2,1)} %bitcast.8, s32[4,4]{1,0:T(4,128)} %bitcast.11), custom_call_target="tpu_custom_call" | custom-call | tf_op jit(solution)/shard_map/layer/pallas_call | solution.py:530
  100.8 0.9 copy.8
  101.6 1.1 %copy.9 = bf16[1408,528]{0,1:T(8,128)(2,1)} copy(bf16[1408,528]{0,1:T(8,128)(2,1)S(1)} %bitcast.6) | data formatting | bytes 2973696
